TPU v7x, 512 devices: a whole 4x8x8 slice. The times are simulated.
512 devices in a mesh: ctx: 64 (over x, y, core), head: 8 (over z).
Axes of the slice: x: 4, y: 8, z: 8, core: 2. Of those that a mesh axis runs over, the one named last changes fastest.
Arguments:
- placement: int32 [64], replicated, may hold values from 0 to 63, each once
- placed_queries: bfloat16 [16384, 4096], P('ctx', 'head'), may hold values from -160 to 160
- placed_keys: bfloat16 [16384, 1024], P('ctx', 'head'), may hold values from -4.5 to 4.5
- placed_values: bfloat16 [16384, 1024], P('ctx', 'head'), may hold values from -6 to 6
- out_weight: bfloat16 [4096, 4096], P('head', 'ctx'), may hold values from -0.25 to 0.25
Outputs:
- attention_out: bfloat16 [16384, 4096], P('ctx', 'head')
Inputs may be any that keep to these rules, and one draw needn't show every extreme that they name: placement holds each of 0 .. 63 once.
All inputs are finite; a program needn't handle non-finite values.
Results may differ from a plain program's by a relative error of at most 0.015.
Values may be sent and summed in bfloat16 or wider, within the bound.
No kernel may reach another device: no remote copies, remote signals or barrier semaphores. Data moves between devices by JAX's collectives and lax.ppermute only.
A program may use at most 64 MiB of HBM per device.

v0:
```python
import jax
import jax.numpy as jnp
from jax import lax
from jax.sharding import PartitionSpec as P

HEAD_FEATURES = 128


masked_score = -1e30


def position_lookup(placement, device_ids):
    table = jnp.arange(placement.shape[0], dtype=jnp.int32)
    matches = device_ids[..., None] == table
    return jnp.sum(jnp.where(matches, placement, 0), axis=-1)


def attend(queries, positions, row_groups, placement, placed_keys, placed_values):
    total_rows = queries.shape[0]
    home_rows = placed_keys.shape[0]
    kv_heads = placed_keys.shape[1] // HEAD_FEATURES
    common_across = queries.shape[1] // placed_keys.shape[1]
    group_rows = total_rows // row_groups
    query_grid = queries.reshape(total_rows, kv_heads, common_across, HEAD_FEATURES)
    score_scale = HEAD_FEATURES ** (-0.5)
    initial = tuple(
        (
            (
                jnp.full((kv_heads, common_across, group_rows), masked_score, jnp.float32),
                jnp.zeros((kv_heads, common_across, group_rows), jnp.float32),
                jnp.zeros((kv_heads, common_across, group_rows, HEAD_FEATURES), jnp.float32),
            )
            for member in range(row_groups)
        )
    )

    def update(current, part_queries, part_positions, key_block, value_block, key_positions):
        running_max, running_sum, running_out = current
        scores = (
            jnp.einsum(
                "rkgd,skd->kgrs", part_queries, key_block, preferred_element_type=jnp.float32
            )
            * score_scale
        )
        allowed = key_positions[None, :] <= part_positions[:, None]
        scores = jnp.where(allowed, scores, masked_score)
        new_max = jnp.maximum(running_max, jnp.max(scores, axis=-1))
        weights = jnp.where(allowed, jnp.exp(scores - new_max[..., None]), 0.0)
        shrink = jnp.exp(running_max - new_max)
        new_sum = running_sum * shrink + jnp.sum(weights, axis=-1)
        new_out = running_out * shrink[..., None] + jnp.einsum(
            "kgrs,skd->kgrd",
            weights.astype(jnp.bfloat16),
            value_block,
            preferred_element_type=jnp.float32,
        )
        return (new_max, new_sum, new_out)

    key_piece = lax.all_gather(placed_keys, "ctx", axis=0, tiled=True)
    value_piece = lax.all_gather(placed_values, "ctx", axis=0, tiled=True)
    count = key_piece.shape[0]
    block_count = count // home_rows
    key_grid = key_piece.reshape(block_count, home_rows, kv_heads, HEAD_FEATURES)
    value_grid = value_piece.reshape(block_count, home_rows, kv_heads, HEAD_FEATURES)
    offsets = jnp.arange(block_count, dtype=jnp.int32) * home_rows

    def one_block(states, operands):
        key_block, value_block, block_first = operands
        key_index = block_first + jnp.arange(home_rows, dtype=jnp.int32)
        key_positions = (
            position_lookup(placement, key_index // home_rows) * home_rows + key_index % home_rows
        )
        earliest = jnp.min(key_positions)
        updated = [
            lax.cond(
                earliest <= jnp.max(positions),
                lambda current: update(
                    current, query_grid, positions, key_block, value_block, key_positions
                ),
                lambda current: current,
                states[0],
            )
        ]
        return (tuple(updated), None)

    finished, unused = lax.scan(one_block, initial, (key_grid, value_grid, offsets))
    outputs = [member_state[2] / member_state[1][..., None] for member_state in finished]
    joined = outputs[0]
    return (
        jnp.transpose(joined, (2, 0, 1, 3))
        .reshape(total_rows, queries.shape[1])
        .astype(jnp.bfloat16)
    )


def softmax_mixer(placement, placed_queries, placed_keys, placed_values):
    home_rows = placed_queries.shape[0]
    own_index = lax.axis_index("ctx")
    own_block = position_lookup(placement, own_index)
    positions = own_block * home_rows + jnp.arange(home_rows, dtype=jnp.int32)
    return attend(placed_queries, positions, 1, placement, placed_keys, placed_values)


def body(placement, placed_queries, placed_keys, placed_values, out_weight):
    hidden = softmax_mixer(placement, placed_queries, placed_keys, placed_values)
    partial_sum = jnp.dot(
        hidden,
        lax.all_gather(out_weight, "ctx", axis=1, tiled=True),
        preferred_element_type=jnp.float32,
    )
    rounded_term = lax.optimization_barrier(partial_sum.astype(jnp.bfloat16)).astype(jnp.float32)
    return lax.psum_scatter(
        rounded_term.astype(jnp.bfloat16), "head", scatter_dimension=1, tiled=True
    )


def solution(mesh):
    placed = (P(), P("ctx", "head"), P("ctx", "head"), P("ctx", "head"), P("head", "ctx"))
    return jax.shard_map(
        body, mesh=mesh, in_specs=placed, out_specs=P("ctx", "head"), check_vma=False
    )
```

profile of v0, /device:TPU:4, one launch (start us, length us, event | category | flops | bytes accessed | tf_op | source)
XLA Modules:
  0.0 730.1 jit_solution(3870190778058489720)
XLA Ops:
  12.7 85.6 %all-gather.4.cloned.1.call-done = bf16[16384,128]{1,0:T(8,128)(2,1)} async-done(((bf16[256,128]{1,0:T(8,128)(2,1)}), bf16[16384,128]{1,0:T(8,128)(2,1)}) %all-gather.4.cloned.1.call-update) | async-done | bytes 4194320 | tf_op jit(solution)/shard_map/all_gather | solution.py:59
  98.3 85.2 %all-gather.6.cloned.1.call-done = bf16[16384,128]{1,0:T(8,128)(2,1)} async-done(((bf16[256,128]{1,0:T(8,128)(2,1)}), bf16[16384,128]{1,0:T(8,128)(2,1)}) %all-gather.6.cloned.1.call-update) | async-done | bytes 4194320 | tf_op jit(solution)/shard_map/all_gather | solution.py:60
  183.6 492.1 %while.17 = (s32[]{:T(128)}, f32[1,4,256]{2,1,0:T(4,128)S(1)}, f32[1,4,256]{2,1,0:T(4,128)S(1)}, f32[1,4,256,128]{3,2,1,0:T(8,128)S(1)}, s32[64]{0:T(128)S(1)}, ...) while((s32[]{:T(128)}, f32[1,4,256]{2,1,0:T(4,128)S(1)}, ...), condition=%wide.region_9.10_spmd.clone, body=%wide.region_2.9_spmd.clone.sunk | while | flops 136964864 | bytes 4927015 | solution.py:86
  188.3 2.9 conditional.3
  211.4 2.9 conditional.3
  226.7 2.9 conditional.3
  234.4 2.9 conditional.3
  242.1 2.9 conditional.3
  249.8 2.9 conditional.3
  265.2 2.9 conditional.3
  280.6 2.9 conditional.3
  288.3 2.9 conditional.3
  296.0 2.9 conditional.3
  303.6 2.9 conditional.3
  311.3 2.9 conditional.3
  319.0 2.9 conditional.3
  326.7 2.9 conditional.3
  334.4 2.9 conditional.3
  342.1 2.9 conditional.3
  349.8 2.9 conditional.3
  357.5 2.9 conditional.3
  365.1 2.9 conditional.3
  372.8 2.9 conditional.3
  380.5 2.9 conditional.3
  388.2 2.9 conditional.3
  395.9 2.9 conditional.3
  403.6 2.9 conditional.3
  411.3 2.9 conditional.3
  419.0 2.9 conditional.3
  426.7 2.9 conditional.3
  434.3 2.9 conditional.3
  442.0 2.9 conditional.3
  449.7 2.9 conditional.3
  457.4 2.9 conditional.3
  465.1 2.9 conditional.3
  472.8 2.9 conditional.3
  480.5 2.9 conditional.3
  488.2 2.9 conditional.3
  495.8 2.9 conditional.3
  503.5 2.9 conditional.3
  511.2 2.9 conditional.3
  518.9 2.9 conditional.3
  526.6 2.9 conditional.3
  534.3 2.9 conditional.3
  542.0 2.9 conditional.3
  549.7 2.9 conditional.3
  557.4 2.9 conditional.3
  565.0 2.9 conditional.3
  572.7 2.9 conditional.3
  580.4 2.9 conditional.3
  588.1 2.9 conditional.3
  595.8 2.9 conditional.3
  603.5 2.9 conditional.3
  611.2 2.9 conditional.3
  618.9 2.9 conditional.3
  626.6 2.9 conditional.3
  634.2 2.9 conditional.3
  641.9 2.9 conditional.3
  649.6 2.9 conditional.3
  657.3 2.9 conditional.3
  665.0 2.9 conditional.3
  672.7 2.9 conditional.3
  675.9 4.8 convolution_convert_fusion
  680.8 42.8 %reduce-scatter.2.cloned.1.call-done = bf16[256,512]{1,0:T(8,128)(2,1)} async-done(((bf16[256,4096]{1,0:T(8,128)(2,1)}), bf16[256,512]{1,0:T(8,128)(2,1)}) %reduce-scatter.2.cloned.1.call-update) | async-done | bytes 262160 | tf_op jit(solution)/shard_map/reduce_scatter | solution.py:112
  (856 shorter events, 419.1 us)
Async XLA Ops:
  6.5 91.8 %all-gather.4.cloned.1.call-start = ((), (), s32[]{:S(2)}) async-start(), calls=%async_computation.1 | async-start | bytes 4259840 | tf_op jit(solution)/shard_map/all_gather | solution.py:59
  7.3 176.2 %all-gather.6.cloned.1.call-start = ((), (), s32[]{:S(2)}) async-start(), calls=%async_computation.2 | async-start | bytes 4259840 | tf_op jit(solution)/shard_map/all_gather | solution.py:60
  8.0 667.9 %all-gather.8.cloned.1.call-start = ((), (), s32[]{:S(2)}) async-start(), calls=%async_computation.3 | async-start | bytes 4259840 | tf_op jit(solution)/shard_map/all_gather | solution.py:108
  8.7 714.8 %reduce-scatter.2.cloned.1.call-start = ((), (), s32[]{:S(2)}) async-start(), calls=%async_computation.4 | async-start | bytes 2359296 | tf_op jit(solution)/shard_map/reduce_scatter | solution.py:112
Sparse Core Ops, SparseCore 0:
  10.7 87.5 all-gather.3
  101.7 81.7 all-gather.5
  186.9 81.8 all-gather.7
  680.9 42.6 reduce-scatter.1
where the time goes:
time: 739 us; the launch traced here: 730 us
  waiting for transfers between devices  216 us (29%)
  other arithmetic  198 us (27%)
  matrix products  166 us (22%)
  loops' own time  93.4 us (13%)
  local copies, waits for them, and re-layouts  43.4 us (6%)
  between operations  13.9 us (2%)
    another operation x1, loops' own time, attend(): lax.scan(one_block, initial, (key_grid, value_grid, offsets))  89.6 us
    dot_general x64, matrix products, update(): jnp.einsum('kgrs,skd->kgrd', weights.astype(jnp.bfloat16), value_block, p...  86.2 us
    all_gather x1, waiting for transfers between devices, attend(): key_piece = lax.all_gather(placed_keys, 'ctx', axis=0, tiled=True)  85.6 us
    reduce_min x64, other arithmetic, one_block(): earliest = jnp.min(key_positions)  85.5 us
    all_gather x1, waiting for transfers between devices, attend(): value_piece = lax.all_gather(placed_values, 'ctx', axis=0, tiled=True)  85.2 us
    dot_general x64, matrix products, update(): jnp.einsum('rkgd,skd->kgrs', part_queries, key_block, preferred_element_t...  74.8 us
    reduce_sum x65, other arithmetic, position_lookup(): return jnp.sum(jnp.where(matches, placement, 0), axis=-1)  49.2 us
    reduce_scatter x1, waiting for transfers between devices, body(): lax.psum_scatter(rounded_term.astype(jnp.bfloat16), 'head', scatter_dimen...  42.8 us
  transfers between devices with their start and end apart: 4, of which 3 were waited for; matrix products, arithmetic and copies ran while one was open for 55% of the time, Pallas kernels for 0%

commit v1 on v0

v1 whole, which is shorter than its diff:
```python
import functools

import jax
import jax.numpy as jnp
from jax import lax
from jax.experimental import pallas as pl
from jax.experimental.pallas import tpu as pltpu
from jax.sharding import PartitionSpec as P

HEAD_FEATURES = 128
CHUNK_BLOCKS = 4
MASKED = -1e30
LOG2_E = 1.4426950408889634


def attend_kernel(blocks, rows, heads, groups, place_ref, q_ref, all_ref, out_ref,
                  order, kv, wt, top, total, acc, hidden, kv_sem, wt_sem):
    features = HEAD_FEATURES
    width = 2 * features
    weight_rows = wt.shape[1]
    factor = features ** (-0.5) * LOG2_E
    own = place_ref[lax.axis_index("ctx")]
    last_chunk = own // CHUNK_BLOCKS
    held = (last_chunk + 1) * CHUNK_BLOCKS

    @pl.loop(0, blocks)
    def _(j):
        order[place_ref[j]] = j

    def fetch(p):
        return pltpu.make_async_copy(
            all_ref.at[order[p], pl.ds(0, rows), :], kv.at[p], kv_sem.at[p]
        )

    @pl.loop(0, held)
    def _(p):
        fetch(p).start()

    weight_copy = pltpu.make_async_copy(
        all_ref.at[:, pl.ds(rows, weight_rows), :], wt, wt_sem
    )
    weight_copy.start()

    top[...] = jnp.full_like(top, MASKED)
    total[...] = jnp.zeros_like(total)
    acc[...] = jnp.zeros_like(acc)
    chunk_rows = CHUNK_BLOCKS * rows

    def step(chunk, masked):
        for i in range(CHUNK_BLOCKS):
            fetch(chunk * CHUNK_BLOCKS + i).wait()
        keys = kv[pl.ds(chunk * CHUNK_BLOCKS, CHUNK_BLOCKS), :, 0:features].reshape(
            chunk_rows, features
        )
        values = kv[pl.ds(chunk * CHUNK_BLOCKS, CHUNK_BLOCKS), :, features:width].reshape(
            chunk_rows, features
        )
        for g in range(heads):
            scores = lax.dot_general(
                q_ref[:, g * features:(g + 1) * features], keys,
                (((1,), (1,)), ((), ())), preferred_element_type=jnp.float32,
            )
            if masked:
                key_at = chunk * chunk_rows + lax.broadcasted_iota(
                    jnp.int32, scores.shape, 1)
                row_at = own * rows + lax.broadcasted_iota(jnp.int32, scores.shape, 0)
                allowed = key_at <= row_at
                scores = jnp.where(allowed, scores, MASKED)
            before = top[g]
            now = jnp.maximum(before, jnp.max(scores, axis=1, keepdims=True))
            top[g] = now
            weights = jnp.exp2((scores - jnp.tile(now, (1, chunk_rows // features))) * factor)
            if masked:
                weights = jnp.where(allowed, weights, 0.0)
            shrink = jnp.exp2((before - now) * factor)
            total[g] = total[g] * shrink + jnp.sum(weights, axis=1, keepdims=True)
            acc[g] = acc[g] * shrink + jnp.dot(
                weights.astype(jnp.bfloat16), values, preferred_element_type=jnp.float32
            )

    @pl.loop(0, last_chunk)
    def _(chunk):
        step(chunk, False)

    step(last_chunk, True)

    for g in range(heads):
        hidden[:, g * features:(g + 1) * features] = (acc[g] / total[g]).astype(jnp.bfloat16)

    weight_copy.wait()
    part_blocks = blocks // groups
    part_rows = weight_rows // 2
    for t in range(groups):
        term = None
        for half in range(2):
            piece = wt[t * part_blocks:(t + 1) * part_blocks,
                       half * part_rows:(half + 1) * part_rows, :].reshape(
                part_blocks * part_rows, width)
            product = lax.dot_general(
                hidden[:, half * width:(half + 1) * width], piece,
                (((1,), (1,)), ((), ())), preferred_element_type=jnp.float32,
            )
            term = product if term is None else term + product
        out_ref[t] = term.astype(jnp.bfloat16)


def body(placement, queries, keys, values, out_weight):
    rows, columns = queries.shape
    blocks = placement.shape[0]
    heads = columns // HEAD_FEATURES
    groups = lax.axis_size("head")
    width = 2 * HEAD_FEATURES
    turned = out_weight.T
    sent = jnp.concatenate(
        [jnp.concatenate([keys, values], 1), turned[:, :width], turned[:, width:]], 0
    )
    weight_rows = 2 * turned.shape[0]
    gathered = lax.all_gather(sent, "ctx", axis=0)
    out_columns = blocks * turned.shape[0] // groups
    terms = pl.pallas_call(
        functools.partial(attend_kernel, blocks, rows, heads, groups),
        out_shape=jax.ShapeDtypeStruct((groups, rows, out_columns), jnp.bfloat16),
        in_specs=[
            pl.BlockSpec(memory_space=pltpu.SMEM),
            pl.BlockSpec(memory_space=pltpu.VMEM),
            pl.BlockSpec(memory_space=pl.ANY),
        ],
        out_specs=pl.BlockSpec(memory_space=pltpu.VMEM),
        scratch_shapes=[
            pltpu.SMEM((blocks,), jnp.int32),
            pltpu.VMEM((blocks, rows, width), jnp.bfloat16),
            pltpu.VMEM((blocks, weight_rows, width), jnp.bfloat16),
            pltpu.VMEM((heads, rows, HEAD_FEATURES), jnp.float32),
            pltpu.VMEM((heads, rows, HEAD_FEATURES), jnp.float32),
            pltpu.VMEM((heads, rows, HEAD_FEATURES), jnp.float32),
            pltpu.VMEM((rows, columns), jnp.bfloat16),
            pltpu.SemaphoreType.DMA((blocks,)),
            pltpu.SemaphoreType.DMA,
        ],
        compiler_params=pltpu.CompilerParams(vmem_limit_bytes=48 * 1024 * 1024),
        name="attend",
    )(placement, queries, gathered)
    return lax.psum_scatter(
        terms.reshape(groups * rows, out_columns), "head", scatter_dimension=0, tiled=True
    )


def solution(mesh):
    placed = (P(), P("ctx", "head"), P("ctx", "head"), P("ctx", "head"), P("head", "ctx"))
    return jax.shard_map(
        body, mesh=mesh, in_specs=placed, out_specs=P("ctx", "head"), check_vma=False
    )
```

time: 739 us -> 200 us (0.27)
  the two profiles are of different devices: /device:TPU:4 before, /device:TPU:8 now
where the time goes in v1:
time: 200 us
  waiting for transfers between devices  172 us (86%)
  between operations  13.4 us (7%)
  Pallas kernels  10 us (5%)
  local copies, waits for them, and re-layouts  2.38 us (1%)
    all_gather x1, waiting for transfers between devices, body(): gathered = lax.all_gather(sent, 'ctx', axis=0)  101 us
    reduce_scatter x1, waiting for transfers between devices, body(): lax.psum_scatter(terms.reshape(groups * rows, out_columns), 'head', scatt...  71.3 us
    pallas_call x1, Pallas kernels, body(): pl.pallas_call(functools.partial(attend_kernel, blocks, rows, heads, grou...  10 us
  transfers between devices with their start and end apart: 2, of which 2 were waited for; matrix products, arithmetic and copies ran while one was open for 0% of the time, Pallas kernels for 0%

profile of v1, /device:TPU:8, one launch (start us, length us, event | category | flops | bytes accessed | tf_op | source)
XLA Modules:
  0.0 199.8 jit_solution(13498480956023769034)
XLA Ops:
  6.5 0.0 all-gather.3.cloned.1.call-start
  6.5 0.8 fusion
  7.3 1.6 pad_maximum_fusion
  8.9 0.0 all-gather.3.cloned.1.call-update
  8.9 0.0 reduce-scatter.2.cloned.1.call-start
  9.0 101.1 %all-gather.3.cloned.1.call-done = bf16[24576,256]{1,0:T(8,128)(2,1)} async-done(((bf16[384,256]{1,0:T(8,128)(2,1)}), bf16[24576,256]{1,0:T(8,128)(2,1)}) %all-gather.3.cloned.1.call-update) | async-done | bytes 12582928 | tf_op jit(solution)/shard_map/all_gather | solution.py:118
  110.0 0.0 copy-start
  110.0 0.9 copy-done
  111.0 0.0 copy-start.1
  111.0 0.7 copy-done.1
  111.6 10.0 %attend.1 = bf16[8,256,512]{2,1,0:T(8,128)(2,1)} custom-call(s32[64]{0:T(128)S(1)} %copy-done.1, bf16[256,512]{1,0:T(8,128)(2,1)S(1)} %copy-done, bf16[64,384,256]{2,1,0:T(8,128)(2,1)} %bitcast.3), custom_call_target="tpu_custom_call" | custom-call | tf_op jit(solution)/shard_map/attend/pallas_call | solution.py:120
  121.6 0.0 reduce-scatter.2.cloned.1.call-update
  121.7 71.3 %reduce-scatter.2.cloned.1.call-done = bf16[256,512]{1,0:T(8,128)(2,1)} async-done(((bf16[2048,512]{1,0:T(8,128)(2,1)}), bf16[256,512]{1,0:T(8,128)(2,1)}) %reduce-scatter.2.cloned.1.call-update) | async-done | bytes 262160 | tf_op jit(solution)/shard_map/reduce_scatter | solution.py:143
Async XLA Ops:
  6.5 103.5 %all-gather.3.cloned.1.call-start = ((), (), s32[]{:S(2)}) async-start(), calls=%async_computation.2 | async-start | bytes 12779520 | tf_op jit(solution)/shard_map/all_gather | solution.py:118
  8.9 184.0 %reduce-scatter.2.cloned.1.call-start = ((), (), s32[]{:S(2)}) async-start(), calls=%async_computation.1 | async-start | bytes 2359296 | tf_op jit(solution)/shard_map/reduce_scatter | solution.py:143
  110.0 0.9 copy-start
  111.0 0.7 copy-start.1
Sparse Core Ops, SparseCore 0:
  10.7 99.3 all-gather.2
  121.8 71.1 reduce-scatter.1

commit v2 on v1

v2 whole, which is shorter than its diff:
```python
import functools

import jax
import jax.numpy as jnp
from jax import lax
from jax.experimental import pallas as pl
from jax.experimental.pallas import tpu as pltpu
from jax.sharding import PartitionSpec as P

HEAD_FEATURES = 128
MASKED = -1e30
LOG2_E = 1.4426950408889634
FACTOR = HEAD_FEATURES ** (-0.5) * LOG2_E
X_SIZE, Y_SIZE, CORES = 4, 8, 2
PEERS = X_SIZE * CORES
SLOTS = Y_SIZE * CORES
STAT_ROWS = 16


def ctx_of(x, y, core):
    return (x * Y_SIZE + y) * CORES + core


Y_GROUPS = [[ctx_of(x, y, c) for y in range(Y_SIZE)] for x in range(X_SIZE) for c in range(CORES)]
XC_GROUPS = [[ctx_of(x, y, c) for x in range(X_SIZE) for c in range(CORES)] for y in range(Y_SIZE)]


def pack_kernel(key_ref, value_ref, weight_ref, out_ref):
    rows, features = key_ref.shape
    half = rows // 2
    count = weight_ref.shape[0]
    width = out_ref.shape[1]
    out_ref[0:half, 0:features] = key_ref[0:half, :]
    out_ref[0:half, features:width] = key_ref[half:rows, :]
    out_ref[half:rows, :] = value_ref[...].astype(jnp.float32).T.astype(jnp.bfloat16)
    for i in range(2):
        out_ref[rows + i * count:rows + (i + 1) * count, :] = (
            weight_ref[:, i * width:(i + 1) * width])


def attend_kernel(rows, heads, place_ref, q_ref, line_ref, other_ref, out_ref,
                  listed, kv, top, total, acc, kv_sem):
    features = HEAD_FEATURES
    half = rows // 2
    me = lax.axis_index("ctx")
    core = lax.rem(me, CORES)
    y = lax.rem(lax.div(me, CORES), Y_SIZE)
    x = lax.div(me, CORES * Y_SIZE)

    copies = [
        pltpu.make_async_copy(
            line_ref.at[:, pl.ds(0, rows), :], kv.at[pl.ds(0, Y_SIZE)], kv_sem.at[0]),
        pltpu.make_async_copy(other_ref, kv.at[pl.ds(Y_SIZE, Y_SIZE)], kv_sem.at[1]),
    ]
    for copy in copies:
        copy.start()
    for copy in copies:
        copy.wait()

    def step(s, slots, masked):
        keys = jnp.concatenate(
            [kv[slot, 0:half, p * features:(p + 1) * features] for slot in slots for p in (0, 1)], 0)
        values = jnp.concatenate([kv[slot, half:rows, :] for slot in slots], 1)

        def scores_of(t):
            scores = lax.dot_general(
                keys, q_ref[s, :, t * features:(t + 1) * features],
                (((1,), (1,)), ((), ())), preferred_element_type=jnp.float32,
            )
            if masked:
                scores = jnp.where(causal(scores.shape), scores, MASKED)
            return scores

        def causal(shape):
            return (lax.broadcasted_iota(jnp.int32, shape, 0)
                    <= lax.broadcasted_iota(jnp.int32, shape, 1))

        def absorb(t, scores):
            lanes = slice(t * rows, (t + 1) * rows)
            before = top[:, lanes]
            now = jnp.maximum(before, jnp.max(scores, axis=0, keepdims=True))
            top[:, lanes] = now
            weights = jnp.exp2((scores - now[0:1]) * FACTOR)
            if masked:
                weights = jnp.where(causal(scores.shape), weights, 0.0)
            shrink = jnp.exp2((before - now) * FACTOR)
            total[:, lanes] = total[:, lanes] * shrink + jnp.sum(weights, axis=0, keepdims=True)
            acc[:, lanes] = acc[:, lanes] * shrink[0:1] + jnp.dot(
                values, weights.astype(jnp.bfloat16), preferred_element_type=jnp.float32)

        scores = scores_of(0)
        for t in range(heads):
            following = scores_of(t + 1) if t + 1 < heads else None
            absorb(t, scores)
            scores = following

    @pl.loop(0, PEERS)
    def _(s):
        query_x = lax.div(s, CORES)
        query_core = lax.rem(s, CORES)
        query_at = place_ref[ctx_of(query_x, y, query_core)]

        def note(i, found):
            slot_core = jnp.where(i < Y_SIZE, core, 1 - core)
            key_at = place_ref[ctx_of(x, lax.rem(i, Y_SIZE), slot_core)]
            listed[found] = i
            return found + (key_at < query_at).astype(jnp.int32)

        found = lax.fori_loop(0, SLOTS, note, jnp.int32(0))
        top[...] = jnp.full_like(top, MASKED)
        total[...] = jnp.zeros_like(total)
        acc[...] = jnp.zeros_like(acc)

        @pl.when(query_x == x)
        def _():
            step(s, [jnp.where(query_core == core, y, Y_SIZE + y)], True)

        fours = lax.div(found, 4)

        @pl.loop(0, fours)
        def _(i):
            step(s, [listed[4 * i + j] for j in range(4)], False)

        rest = found - 4 * fours

        @pl.when(rest >= 2)
        def _():
            step(s, [listed[4 * fours], listed[4 * fours + 1]], False)

        @pl.when(lax.rem(rest, 2) == 1)
        def _():
            step(s, [listed[found - 1]], False)

        row = lax.broadcasted_iota(jnp.int32, (STAT_ROWS, rows), 0)
        stats = jnp.zeros((STAT_ROWS, rows), jnp.float32)
        for t in range(heads):
            lanes = slice(t * rows, (t + 1) * rows)
            norm = jnp.maximum(total[0:1, lanes], 1e-30)
            out_ref[s, t * features:(t + 1) * features, :] = (
                acc[:, lanes] * (1.0 / norm)).astype(jnp.bfloat16)
            left = top[0:1, lanes] * FACTOR + jnp.log(norm) * LOG2_E
            for part in range(3):
                piece = left.astype(jnp.bfloat16).astype(jnp.float32)
                stats = jnp.where(row == 3 * t + part, piece, stats)
                left = left - piece
        out_ref[s, heads * features:heads * features + STAT_ROWS, :] = stats.astype(jnp.bfloat16)


def merge_kernel(heads, groups, part_ref, weight_ref, out_ref, hidden, weight, sems):
    features = HEAD_FEATURES
    width = 2 * features
    copies = [
        pltpu.make_async_copy(
            weight_ref.at[x * CORES + c], weight.at[x, :, c], sems.at[x * CORES + c])
        for x in range(X_SIZE) for c in range(CORES)
    ]
    for copy in copies:
        copy.start()

    stats = [
        part_ref[j, heads * features:heads * features + STAT_ROWS, :].astype(jnp.float32)
        for j in range(PEERS)
    ]
    for c in range(CORES):
        for t in range(heads):
            peers = [i * CORES + c for i in range(X_SIZE)]
            levels = [
                stats[j][3 * t:3 * t + 1] + stats[j][3 * t + 1:3 * t + 2]
                + stats[j][3 * t + 2:3 * t + 3]
                for j in peers
            ]
            peak = functools.reduce(jnp.maximum, levels)
            shares = [jnp.exp2(level - peak) for level in levels]
            inverse = 1.0 / sum(shares)
            merged = sum(
                part_ref[j, t * features:(t + 1) * features, :].astype(jnp.float32)
                * (share * inverse)
                for j, share in zip(peers, shares)
            )
            at = (c * heads + t) * features
            hidden[:, at:at + features] = merged.T.astype(jnp.bfloat16)

    for copy in copies:
        copy.wait()
    lines = X_SIZE * Y_SIZE // groups
    parts = Y_SIZE // lines
    part_rows = weight.shape[3] // 2
    for g in range(groups):
        term = None
        for side in range(2):
            start = (g % parts) * lines
            piece = weight[g // parts, start:start + lines, :,
                           side * part_rows:(side + 1) * part_rows, :].reshape(
                lines * CORES * part_rows, width)
            product = lax.dot_general(
                hidden[:, side * width:(side + 1) * width], piece,
                (((1,), (1,)), ((), ())), preferred_element_type=jnp.float32,
            )
            term = product if term is None else term + product
        out_ref[g] = term.astype(jnp.bfloat16)


def hold(array):
    return pl.pallas_call(
        lambda array_ref, out_ref: None,
        out_shape=jax.ShapeDtypeStruct(array.shape, array.dtype),
        in_specs=[pl.BlockSpec(memory_space=pl.ANY)],
        out_specs=pl.BlockSpec(memory_space=pl.ANY),
        input_output_aliases={0: 0},
        name="hold",
    )(array)


def body(placement, queries, keys, values, out_weight):
    rows, columns = queries.shape
    blocks = placement.shape[0]
    width = 2 * HEAD_FEATURES
    heads = columns // HEAD_FEATURES // CORES
    groups = lax.axis_size("head")

    turned = out_weight.T
    sent = pl.pallas_call(
        pack_kernel,
        out_shape=jax.ShapeDtypeStruct((rows + 2 * turned.shape[0], width), jnp.bfloat16),
        in_specs=[pl.BlockSpec(memory_space=pltpu.VMEM)] * 3,
        out_specs=pl.BlockSpec(memory_space=pltpu.VMEM),
        name="pack",
    )(keys, values, turned)
    line = lax.all_gather(sent, "ctx", axis=0, axis_index_groups=Y_GROUPS)

    asked = jnp.stack([queries[:, c * width:(c + 1) * width] for c in range(CORES)], 0)
    asked = jnp.broadcast_to(asked[None], (X_SIZE,) + asked.shape).reshape(PEERS, rows, width)
    asked = lax.all_to_all(asked, "ctx", 0, 0, tiled=True, axis_index_groups=XC_GROUPS)
    asked = hold(asked)
    other = lax.ppermute(line[:, :rows], "ctx", [(i, i ^ 1) for i in range(blocks)])
    weights = lax.all_gather(line[:, rows:], "ctx", axis=0, axis_index_groups=XC_GROUPS)

    parts = pl.pallas_call(
        functools.partial(attend_kernel, rows, heads),
        out_shape=jax.ShapeDtypeStruct((PEERS, width + STAT_ROWS, rows), jnp.bfloat16),
        in_specs=[
            pl.BlockSpec(memory_space=pltpu.SMEM),
            pl.BlockSpec(memory_space=pltpu.VMEM),
            pl.BlockSpec(memory_space=pl.ANY),
            pl.BlockSpec(memory_space=pl.ANY),
        ],
        out_specs=pl.BlockSpec(memory_space=pltpu.VMEM),
        scratch_shapes=[
            pltpu.SMEM((SLOTS + 1,), jnp.int32),
            pltpu.VMEM((SLOTS, rows, width), jnp.bfloat16),
            pltpu.VMEM((8, heads * rows), jnp.float32),
            pltpu.VMEM((8, heads * rows), jnp.float32),
            pltpu.VMEM((HEAD_FEATURES, heads * rows), jnp.float32),
            pltpu.SemaphoreType.DMA((2,)),
        ],
        compiler_params=pltpu.CompilerParams(
            vmem_limit_bytes=32 * 1024 * 1024),
        cost_estimate=pl.CostEstimate(
            flops=9_000_000_000, transcendentals=9_000_000, bytes_accessed=5_000_000),
        name="attend",
    )(placement, asked, line, other)

    gathered = lax.all_to_all(parts, "ctx", 0, 0, tiled=True, axis_index_groups=XC_GROUPS)

    out_columns = blocks * turned.shape[0] // groups
    weight_shape = (X_SIZE, Y_SIZE, CORES) + (2 * turned.shape[0], width)
    terms = pl.pallas_call(
        functools.partial(merge_kernel, heads, groups),
        out_shape=jax.ShapeDtypeStruct((groups, rows, out_columns), jnp.bfloat16),
        in_specs=[
            pl.BlockSpec(memory_space=pltpu.VMEM),
            pl.BlockSpec(memory_space=pl.ANY),
        ],
        out_specs=pl.BlockSpec(memory_space=pltpu.VMEM),
        scratch_shapes=[
            pltpu.VMEM((rows, columns), jnp.bfloat16),
            pltpu.VMEM(weight_shape, jnp.bfloat16),
            pltpu.SemaphoreType.DMA((PEERS,)),
        ],
        compiler_params=pltpu.CompilerParams(vmem_limit_bytes=32 * 1024 * 1024),
        name="merge_project",
    )(gathered, weights)
    return lax.psum_scatter(
        terms.reshape(groups * rows, out_columns), "head", scatter_dimension=0, tiled=True
    )


def solution(mesh):
    placed = (P(), P("ctx", "head"), P("ctx", "head"), P("ctx", "head"), P("head", "ctx"))

    return jax.shard_map(
        body, mesh=mesh, in_specs=placed, out_specs=P("ctx", "head"), check_vma=False
    )
```

time: 200 us -> 187 us (0.935)
  the two profiles are of different devices: /device:TPU:8 before, /device:TPU:10 now
where the time goes in v2:
time: 187 us
  waiting for transfers between devices  90.2 us (48%)
  blocking collectives  42.8 us (23%)
  Pallas kernels  32.1 us (17%)
  between operations  13.2 us (7%)
  local copies, waits for them, and re-layouts  6.57 us (4%)
  starting transfers between devices  1.99 us (1%)
    all_gather x1, waiting for transfers between devices, body(): line = lax.all_gather(sent, 'ctx', axis=0, axis_index_groups=Y_GROUPS)  47.4 us
    reduce_scatter x1, waiting for transfers between devices, body(): lax.psum_scatter(terms.reshape(groups * rows, out_columns), 'head', scatt...  42.7 us
    pallas_call x1, Pallas kernels, body(): pl.pallas_call(functools.partial(attend_kernel, rows, heads), out_shape=j...  27.1 us
    all_to_all x1, blocking collectives, body(): lax.all_to_all(asked, 'ctx', 0, 0, tiled=True, axis_index_groups=XC_GROUPS)  24.4 us
    all_to_all x1, blocking collectives, body(): lax.all_to_all(parts, 'ctx', 0, 0, tiled=True, axis_index_groups=XC_GROUPS)  18.4 us
  transfers between devices with their start and end apart: 4, of which 2 were waited for; matrix products, arithmetic and copies ran while one was open for 1% of the time, Pallas kernels for 15%

profile of v2, /device:TPU:10, one launch (start us, length us, event | category | flops | bytes accessed | tf_op | source)
XLA Modules:
  0.0 186.8 jit_solution(4721849670966125242)
XLA Ops:
  6.5 0.0 all-gather.5.cloned.1.call-start
  6.5 1.7 pack.1
  8.2 0.0 all-gather.5.cloned.1.call-update
  8.2 0.0 all-gather.7.cloned.1.call-start
  8.3 47.4 %all-gather.5.cloned.1.call-done = bf16[3072,256]{1,0:T(8,128)(2,1)} async-done(((bf16[384,256]{1,0:T(8,128)(2,1)}), bf16[3072,256]{1,0:T(8,128)(2,1)}) %all-gather.5.cloned.1.call-update) | async-done | bytes 1572880 | tf_op jit(solution)/shard_map/all_gather | solution.py:229
  55.7 0.0 copy-start.2
  55.7 2.0 %slice.17 = bf16[8,128,256]{2,1,0:T(8,128)(2,1)} slice(bf16[8,384,256]{2,1,0:T(8,128)(2,1)} %bitcast.10), slice={[0:8], [256:384], [0:256]} | slice | bytes 1048576 | tf_op jit(solution)/shard_map/slice | solution.py:236
  57.7 0.0 copy-start.4
  57.7 0.0 all-gather.7.cloned.1.call-update
  57.7 0.0 reduce-scatter.2.cloned.1.call-start
  57.8 0.0 copy-done.2
  57.8 1.0 slice.16
  58.8 1.9 %collective-permute-start = (bf16[8,256,256]{2,1,0:T(8,128)(2,1)}, bf16[8,256,256]{2,1,0:T(8,128)(2,1)S(1)}, u32[]{:S(2)}, u32[]{:S(2)}) collective-permute-start(bf16[8,256,256]{2,1,0:T(8,128)(2,1)} %slice.16), channel_id=1, source_target_pairs={{0,8},{8,0},{16,24},{24,16},{32,40},{40,32},{48,56},{56,48},{64,72... | collective-permute-start | bytes 3145736 | tf_op jit(solution)/shard_map/ppermute | solution.py:235
  60.7 0.0 copy-done.4
  60.8 0.1 broadcast_in_dim.2
  60.9 0.0 copy-start.3
  60.9 24.4 %all_to_all.10.array_ref = bf16[8,256,256]{2,1,0:T(8,128)(2,1)} all-to-all(bf16[8,256,256]{2,1,0:T(8,128)(2,1)S(1)} %bitcast.13), channel_id=1, replica_groups={{0,8,128,136,256,264,384,392},{16,24,144,152,272,280,400,408},{32,40,16..., dimensions={0} | all-to-all | bytes 2097152 | tf_op jit(solution)/shard_map/all_to_all | solution.py:233
  85.3 0.0 collective-permute-done.other_ref
  85.3 0.0 copy-done.3
  85.3 0.0 copy-start.1
  85.3 1.2 copy-done.1
  86.5 27.1 %attend.1 = bf16[8,272,256]{2,1,0:T(8,128)(2,1)S(1)} custom-call(s32[64]{0:T(128)S(1)} %copy-done.3, bf16[8,256,256]{2,1,0:T(8,128)(2,1)S(1)} %copy-done.1, bf16[8,384,256]{2,1,0:T(8,128)(2,1)S(1)} %bitcast.12, bf16[8,256,256]{2,1,0:T(8,128)(2,1)S(1)} %collective-permute-done.other_ref), custom_call_target="tpu_custom_call" | custom-call | flops 8999999488 | bytes 5000000 | tf_op jit(solution)/shard_map/attend/pallas_call | solution.py:238
  113.6 18.4 %all_to_all.11.part_ref = bf16[8,272,256]{2,1,0:T(8,128)(2,1)S(1)} all-to-all(bf16[8,272,256]{2,1,0:T(8,128)(2,1)S(1)} %attend.1), channel_id=1, replica_groups={{0,8,128,136,256,264,384,392},{16,24,144,152,272,280,400,408},{32,40,16..., dimensions={0} | all-to-all | bytes 2228224 | tf_op jit(solution)/shard_map/all_to_all | solution.py:263
  132.0 0.0 all-gather.7.cloned.1.call-done
  132.0 0.0 copy-start
  132.0 2.2 %copy-done = bf16[64,128,256]{2,1,0:T(8,128)(2,1)S(1)} copy-done((bf16[64,128,256]{2,1,0:T(8,128)(2,1)S(1)}, bf16[64,128,256]{2,1,0:T(8,128)(2,1)}, u32[]{:S(2)}) %copy-start) | copy-done | bytes 4194328
  134.2 3.3 %merge_project.1 = bf16[8,256,512]{2,1,0:T(8,128)(2,1)} custom-call(bf16[8,272,256]{2,1,0:T(8,128)(2,1)S(1)} %all_to_all.11.part_ref, bf16[8,8,128,256]{3,2,1,0:T(8,128)(2,1)S(1)} %bitcast.9), custom_call_target="tpu_custom_call" | custom-call | tf_op jit(solution)/shard_map/merge_project/pallas_call | solution.py:267
  137.5 0.0 reduce-scatter.2.cloned.1.call-update
  137.6 42.7 %reduce-scatter.2.cloned.1.call-done = bf16[256,512]{1,0:T(8,128)(2,1)} async-done(((bf16[2048,512]{1,0:T(8,128)(2,1)}), bf16[256,512]{1,0:T(8,128)(2,1)}) %reduce-scatter.2.cloned.1.call-update) | async-done | bytes 262160 | tf_op jit(solution)/shard_map/reduce_scatter | solution.py:283
  (3 shorter events, 0.0 us)
Async XLA Ops:
  6.5 49.2 %all-gather.5.cloned.1.call-start = ((), (), s32[]{:S(2)}) async-start(), calls=%async_computation.4 | async-start | bytes 1769472 | tf_op jit(solution)/shard_map/all_gather | solution.py:229
  8.2 123.8 %all-gather.7.cloned.1.call-start = ((), (), s32[]{:S(2)}) async-start(), calls=%async_computation.5 | async-start | bytes 4718592 | tf_op jit(solution)/shard_map/all_gather | solution.py:236
  55.7 2.1 %copy-start.2 = (bf16[3072,256]{1,0:T(8,128)(2,1)S(1)}, bf16[3072,256]{1,0:T(8,128)(2,1)}, u32[]{:S(2)}) copy-start(bf16[3072,256]{1,0:T(8,128)(2,1)} %all-gather.5.cloned.1.call-done) | copy-start | bytes 4718596
  57.7 3.0 %copy-start.4 = (bf16[256,512]{1,0:T(8,128)(2,1)S(1)}, bf16[256,512]{1,0:T(8,128)(2,1)}, u32[]{:S(2)}) copy-start(bf16[256,512]{1,0:T(8,128)(2,1)} %param.6) | copy-start | bytes 786436
  57.7 122.6 %reduce-scatter.2.cloned.1.call-start = ((), (), s32[]{:S(2)}) async-start(), calls=%async_computation.3 | async-start | bytes 2359296 | tf_op jit(solution)/shard_map/reduce_scatter | solution.py:283
  58.8 26.5 %collective-permute-start = (bf16[8,256,256]{2,1,0:T(8,128)(2,1)}, bf16[8,256,256]{2,1,0:T(8,128)(2,1)S(1)}, u32[]{:S(2)}, u32[]{:S(2)}) collective-permute-start(bf16[8,256,256]{2,1,0:T(8,128)(2,1)} %slice.16), channel_id=1, source_target_pairs={{0,8},{8,0},{16,24},{24,16},{32,40},{40,32},{48,56},{56,48},{64,72... | collective-permute-start | bytes 3145736 | tf_op jit(solution)/shard_map/ppermute | solution.py:235
  60.9 24.4 %copy-start.3 = (s32[64]{0:T(128)S(1)}, s32[64]{0:T(128)}, u32[]{:S(2)}) copy-start(s32[64]{0:T(128)} %place_ref.1) | copy-start | bytes 772
  85.3 1.3 copy-start.1
  132.0 2.2 %copy-start = (bf16[64,128,256]{2,1,0:T(8,128)(2,1)S(1)}, bf16[64,128,256]{2,1,0:T(8,128)(2,1)}, u32[]{:S(2)}) copy-start(bf16[64,128,256]{2,1,0:T(8,128)(2,1)} %all-gather.7.cloned.1.call-done) | copy-start | bytes 12582916
Sparse Core Ops, SparseCore 0:
  9.4 46.2 all-gather.4
  57.8 40.0 all-gather.6
  137.7 42.5 reduce-scatter.1

commit v3 on v2

--- a/solution.py
+++ b/solution.py
@@ -25,21 +25,26 @@
 XC_GROUPS = [[ctx_of(x, y, c) for x in range(X_SIZE) for c in range(CORES)] for y in range(Y_SIZE)]
 
 
-def pack_kernel(key_ref, value_ref, weight_ref, out_ref):
+def pack_kernel(key_ref, value_ref, query_ref, weight_ref, line_ref, ask_ref, column_ref):
     rows, features = key_ref.shape
     half = rows // 2
     count = weight_ref.shape[0]
-    width = out_ref.shape[1]
-    out_ref[0:half, 0:features] = key_ref[0:half, :]
-    out_ref[0:half, features:width] = key_ref[half:rows, :]
-    out_ref[half:rows, :] = value_ref[...].astype(jnp.float32).T.astype(jnp.bfloat16)
+    width = line_ref.shape[1]
+    line_ref[0:half, 0:features] = key_ref[0:half, :]
+    line_ref[0:half, features:width] = key_ref[half:rows, :]
+    line_ref[half:rows, :] = value_ref[...].astype(jnp.float32).T.astype(jnp.bfloat16)
+    for c in range(CORES):
+        piece = query_ref[:, c * width:(c + 1) * width]
+        for x in range(X_SIZE):
+            ask_ref[x * CORES + c] = piece
     for i in range(2):
-        out_ref[rows + i * count:rows + (i + 1) * count, :] = (
-            weight_ref[:, i * width:(i + 1) * width])
-
-
-def attend_kernel(rows, heads, place_ref, q_ref, line_ref, other_ref, out_ref,
-                  listed, kv, top, total, acc, kv_sem):
+        piece = weight_ref[:, i * width:(i + 1) * width]
+        for y in range(Y_SIZE):
+            column_ref[y, i * count:(i + 1) * count, :] = piece
+
+
+def attend_kernel(rows, heads, place_ref, ask_ref, line_ref, other_ref, out_ref,
+                  listed, q_ref, kv, top, total, acc, kv_sem):
     features = HEAD_FEATURES
     half = rows // 2
     me = lax.axis_index("ctx")
@@ -48,9 +53,9 @@
     x = lax.div(me, CORES * Y_SIZE)
 
     copies = [
-        pltpu.make_async_copy(
-            line_ref.at[:, pl.ds(0, rows), :], kv.at[pl.ds(0, Y_SIZE)], kv_sem.at[0]),
+        pltpu.make_async_copy(line_ref, kv.at[pl.ds(0, Y_SIZE)], kv_sem.at[0]),
         pltpu.make_async_copy(other_ref, kv.at[pl.ds(Y_SIZE, Y_SIZE)], kv_sem.at[1]),
+        pltpu.make_async_copy(ask_ref, q_ref, kv_sem.at[2]),
     ]
     for copy in copies:
         copy.start()
@@ -219,42 +224,47 @@
     groups = lax.axis_size("head")
 
     turned = out_weight.T
-    sent = pl.pallas_call(
+    sent, asked, column = pl.pallas_call(
         pack_kernel,
-        out_shape=jax.ShapeDtypeStruct((rows + 2 * turned.shape[0], width), jnp.bfloat16),
-        in_specs=[pl.BlockSpec(memory_space=pltpu.VMEM)] * 3,
-        out_specs=pl.BlockSpec(memory_space=pltpu.VMEM),
+        out_shape=(
+            jax.ShapeDtypeStruct((rows, width), jnp.bfloat16),
+            jax.ShapeDtypeStruct((PEERS, rows, width), jnp.bfloat16),
+            jax.ShapeDtypeStruct((Y_SIZE, 2 * turned.shape[0], width), jnp.bfloat16),
+        ),
+        in_specs=[pl.BlockSpec(memory_space=pltpu.VMEM)] * 4,
+        out_specs=(pl.BlockSpec(memory_space=pltpu.VMEM),) * 3,
         name="pack",
-    )(keys, values, turned)
+    )(keys, values, queries, turned)
     line = lax.all_gather(sent, "ctx", axis=0, axis_index_groups=Y_GROUPS)
 
-    asked = jnp.stack([queries[:, c * width:(c + 1) * width] for c in range(CORES)], 0)
-    asked = jnp.broadcast_to(asked[None], (X_SIZE,) + asked.shape).reshape(PEERS, rows, width)
+    column = lax.all_to_all(column, "ctx", 0, 0, tiled=True, axis_index_groups=Y_GROUPS)
+    column = hold(column)
     asked = lax.all_to_all(asked, "ctx", 0, 0, tiled=True, axis_index_groups=XC_GROUPS)
     asked = hold(asked)
-    other = lax.ppermute(line[:, :rows], "ctx", [(i, i ^ 1) for i in range(blocks)])
-    weights = lax.all_gather(line[:, rows:], "ctx", axis=0, axis_index_groups=XC_GROUPS)
+    other = lax.ppermute(line, "ctx", [(i, i ^ 1) for i in range(blocks)])
+    weights = lax.all_gather(column, "ctx", axis=0, axis_index_groups=XC_GROUPS)
 
     parts = pl.pallas_call(
         functools.partial(attend_kernel, rows, heads),
         out_shape=jax.ShapeDtypeStruct((PEERS, width + STAT_ROWS, rows), jnp.bfloat16),
         in_specs=[
             pl.BlockSpec(memory_space=pltpu.SMEM),
-            pl.BlockSpec(memory_space=pltpu.VMEM),
+            pl.BlockSpec(memory_space=pl.ANY),
             pl.BlockSpec(memory_space=pl.ANY),
             pl.BlockSpec(memory_space=pl.ANY),
         ],
         out_specs=pl.BlockSpec(memory_space=pltpu.VMEM),
         scratch_shapes=[
             pltpu.SMEM((SLOTS + 1,), jnp.int32),
+            pltpu.VMEM((PEERS, rows, width), jnp.bfloat16),
             pltpu.VMEM((SLOTS, rows, width), jnp.bfloat16),
             pltpu.VMEM((8, heads * rows), jnp.float32),
             pltpu.VMEM((8, heads * rows), jnp.float32),
             pltpu.VMEM((HEAD_FEATURES, heads * rows), jnp.float32),
-            pltpu.SemaphoreType.DMA((2,)),
+            pltpu.SemaphoreType.DMA((3,)),
         ],
         compiler_params=pltpu.CompilerParams(
-            vmem_limit_bytes=32 * 1024 * 1024),
+            vmem_limit_bytes=60 * 1024 * 1024),
         cost_estimate=pl.CostEstimate(
             flops=9_000_000_000, transcendentals=9_000_000, bytes_accessed=5_000_000),
         name="attend",
@@ -277,7 +287,7 @@
             pltpu.VMEM(weight_shape, jnp.bfloat16),
             pltpu.SemaphoreType.DMA((PEERS,)),
         ],
-        compiler_params=pltpu.CompilerParams(vmem_limit_bytes=32 * 1024 * 1024),
+        compiler_params=pltpu.CompilerParams(vmem_limit_bytes=60 * 1024 * 1024),
         name="merge_project",
     )(gathered, weights)
     return lax.psum_scatter(

time: 187 us -> 186 us (level)
  the two profiles are of different devices: /device:TPU:10 before, /device:TPU:22 now
where the time goes in v3:
time: 186 us; the launch traced here: 185 us
  waiting for transfers between devices  70.3 us (38%)
  blocking collectives  62.8 us (34%)
  Pallas kernels  36 us (19%)
  between operations  13.1 us (7%)
  starting transfers between devices  1.99 us (1%)
    reduce_scatter x1, waiting for transfers between devices, body(): lax.psum_scatter(terms.reshape(groups * rows, out_columns), 'head', scatt...  48.2 us
    pallas_call x1, Pallas kernels, body(): pl.pallas_call(functools.partial(attend_kernel, rows, heads), out_shape=j...  27.7 us
    all_to_all x1, blocking collectives, body(): lax.all_to_all(column, 'ctx', 0, 0, tiled=True, axis_index_groups=Y_GROUPS)  22.2 us
    all_gather x1, waiting for transfers between devices, body(): line = lax.all_gather(sent, 'ctx', axis=0, axis_index_groups=Y_GROUPS)  22.1 us
    all_to_all x1, blocking collectives, body(): lax.all_to_all(parts, 'ctx', 0, 0, tiled=True, axis_index_groups=XC_GROUPS)  21.8 us
    all_to_all x1, blocking collectives, body(): lax.all_to_all(asked, 'ctx', 0, 0, tiled=True, axis_index_groups=XC_GROUPS)  18.7 us
    pallas_call x1, Pallas kernels, body(): pl.pallas_call(functools.partial(merge_kernel, heads, groups), out_shape=...  6.08 us
  transfers between devices with their start and end apart: 4, of which 2 were waited for; matrix products, arithmetic and copies ran while one was open for 0% of the time, Pallas kernels for 15%

profile of v3, /device:TPU:22, one launch (start us, length us, event | category | flops | bytes accessed | tf_op | source)
XLA Modules:
  0.0 185.3 jit_solution(1497325009871750312)
XLA Ops:
  6.5 0.0 all-gather.5.cloned.1.call-start
  6.5 2.3 %pack.1 = (bf16[256,256]{1,0:T(8,128)(2,1)}, bf16[8,256,256]{2,1,0:T(8,128)(2,1)}, bf16[8,128,256]{2,1,0:T(8,128)(2,1)}) custom-call(bf16[256,128]{1,0:T(8,128)(2,1)} %key_ref.1, bf16[256,128]{1,0:T(8,128)(2,1)} %value_ref.1, bf16[256,512]{1,0:T(8,128)(2,1)} %query_ref.1, bf16[64,512]{1,0:T(8,128)(2,1)} %bitcast.6), custom_call_target="tpu_custom_call" | custom-call | tf_op jit(solution)/shard_map/pack/pallas_call | solution.py:227
  8.8 0.0 copy-start
  8.8 0.0 all-gather.5.cloned.1.call-update
  8.8 0.0 all-gather.7.cloned.1.call-start
  8.9 22.2 %all_to_all.15.array_ref = bf16[8,128,256]{2,1,0:T(8,128)(2,1)} all-to-all(bf16[8,128,256]{2,1,0:T(8,128)(2,1)} %get-tuple-element.10), channel_id=1, replica_groups={{0,16,32,48,64,80,96,112},{8,24,40,56,72,88,104,120},{128,144,160,176,1..., dimensions={0} | all-to-all | bytes 1048576 | tf_op jit(solution)/shard_map/all_to_all | solution.py:240
  31.1 0.0 all-gather.7.cloned.1.call-update
  31.2 0.0 reduce-scatter.2.cloned.1.call-start
  31.2 22.1 %all-gather.5.cloned.1.call-done = bf16[2048,256]{1,0:T(8,128)(2,1)} async-done(((bf16[256,256]{1,0:T(8,128)(2,1)}), bf16[2048,256]{1,0:T(8,128)(2,1)}) %all-gather.5.cloned.1.call-update) | async-done | bytes 1048592 | tf_op jit(solution)/shard_map/all_gather | solution.py:238
  53.3 1.9 %collective-permute-start = (bf16[8,256,256]{2,1,0:T(8,128)(2,1)}, bf16[8,256,256]{2,1,0:T(8,128)(2,1)S(1)}, u32[]{:S(2)}, u32[]{:S(2)}) collective-permute-start(bf16[8,256,256]{2,1,0:T(8,128)(2,1)} %bitcast.7), channel_id=1, source_target_pairs={{0,8},{8,0},{16,24},{24,16},{32,40},{40,32},{48,56},{56,48},{64,72... | collective-permute-start | bytes 3145736 | tf_op jit(solution)/shard_map/ppermute | solution.py:244
  55.2 0.0 copy-done
  55.2 18.7 %all_to_all.16.array_ref = bf16[8,256,256]{2,1,0:T(8,128)(2,1)} all-to-all(bf16[8,256,256]{2,1,0:T(8,128)(2,1)S(1)} %copy-done), channel_id=1, replica_groups={{0,8,128,136,256,264,384,392},{16,24,144,152,272,280,400,408},{32,40,16..., dimensions={0} | all-to-all | bytes 2097152 | tf_op jit(solution)/shard_map/all_to_all | solution.py:242
  73.9 0.0 collective-permute-done.other_ref
  73.9 0.0 copy-start.1
  73.9 1.0 copy-done.1
  74.9 27.7 %attend.1 = bf16[8,272,256]{2,1,0:T(8,128)(2,1)} custom-call(s32[64]{0:T(128)} %place_ref.1, bf16[8,256,256]{2,1,0:T(8,128)(2,1)} %hold.2.ask_ref, bf16[8,256,256]{2,1,0:T(8,128)(2,1)} %bitcast.8, bf16[8,256,256]{2,1,0:T(8,128)(2,1)} %copy-done.1), custom_call_target="tpu_custom_call" | custom-call | flops 8999999488 | bytes 5000000 | tf_op jit(solution)/shard_map/attend/pallas_call | solution.py:247
  102.6 21.8 %all_to_all.17.part_ref = bf16[8,272,256]{2,1,0:T(8,128)(2,1)} all-to-all(bf16[8,272,256]{2,1,0:T(8,128)(2,1)} %attend.1), channel_id=1, replica_groups={{0,8,128,136,256,264,384,392},{16,24,144,152,272,280,400,408},{32,40,16..., dimensions={0} | all-to-all | bytes 2228224 | tf_op jit(solution)/shard_map/all_to_all | solution.py:273
  124.4 0.0 all-gather.7.cloned.1.call-done
  124.4 6.1 %merge_project.1 = bf16[8,256,512]{2,1,0:T(8,128)(2,1)} custom-call(bf16[8,272,256]{2,1,0:T(8,128)(2,1)} %all_to_all.17.part_ref, bf16[8,8,128,256]{3,2,1,0:T(8,128)(2,1)} %bitcast.5), custom_call_target="tpu_custom_call" | custom-call | tf_op jit(solution)/shard_map/merge_project/pallas_call | solution.py:277
  130.5 0.0 reduce-scatter.2.cloned.1.call-update
  130.5 48.2 %reduce-scatter.2.cloned.1.call-done = bf16[256,512]{1,0:T(8,128)(2,1)} async-done(((bf16[2048,512]{1,0:T(8,128)(2,1)}), bf16[256,512]{1,0:T(8,128)(2,1)}) %reduce-scatter.2.cloned.1.call-update) | async-done | bytes 262160 | tf_op jit(solution)/shard_map/reduce_scatter | solution.py:293
  (2 shorter events, 0.0 us)
Async XLA Ops:
  6.5 46.8 %all-gather.5.cloned.1.call-start = ((), (), s32[]{:S(2)}) async-start(), calls=%async_computation.5 | async-start | bytes 1179648 | tf_op jit(solution)/shard_map/all_gather | solution.py:238
  8.8 46.4 %copy-start = (bf16[8,256,256]{2,1,0:T(8,128)(2,1)S(1)}, bf16[8,256,256]{2,1,0:T(8,128)(2,1)}, u32[]{:S(2)}) copy-start(bf16[8,256,256]{2,1,0:T(8,128)(2,1)} %get-tuple-element.8) | copy-start | bytes 3145732
  8.8 115.6 %all-gather.7.cloned.1.call-start = ((), (), s32[]{:S(2)}) async-start(), calls=%async_computation.6 | async-start | bytes 4718592 | tf_op jit(solution)/shard_map/all_gather | solution.py:245
  31.2 147.6 %reduce-scatter.2.cloned.1.call-start = ((), (), s32[]{:S(2)}) async-start(), calls=%async_computation.4 | async-start | bytes 2359296 | tf_op jit(solution)/shard_map/reduce_scatter | solution.py:293
  53.3 20.6 %collective-permute-start = (bf16[8,256,256]{2,1,0:T(8,128)(2,1)}, bf16[8,256,256]{2,1,0:T(8,128)(2,1)S(1)}, u32[]{:S(2)}, u32[]{:S(2)}) collective-permute-start(bf16[8,256,256]{2,1,0:T(8,128)(2,1)} %bitcast.7), channel_id=1, source_target_pairs={{0,8},{8,0},{16,24},{24,16},{32,40},{40,32},{48,56},{56,48},{64,72... | collective-permute-start | bytes 3145736 | tf_op jit(solution)/shard_map/ppermute | solution.py:244
  73.9 1.0 copy-start.1
Sparse Core Ops, SparseCore 0:
  9.4 43.8 all-gather.4
  55.4 36.9 all-gather.6
  130.7 48.0 reduce-scatter.1

commit v4 on v2

--- a/solution.py
+++ b/solution.py
@@ -38,7 +38,7 @@
             weight_ref[:, i * width:(i + 1) * width])
 
 
-def attend_kernel(rows, heads, place_ref, q_ref, line_ref, other_ref, out_ref,
+def attend_kernel(own, rows, heads, place_ref, q_ref, line_ref, other_ref, out_ref,
                   listed, kv, top, total, acc, kv_sem):
     features = HEAD_FEATURES
     half = rows // 2
@@ -50,7 +50,8 @@
     copies = [
         pltpu.make_async_copy(
             line_ref.at[:, pl.ds(0, rows), :], kv.at[pl.ds(0, Y_SIZE)], kv_sem.at[0]),
-        pltpu.make_async_copy(other_ref, kv.at[pl.ds(Y_SIZE, Y_SIZE)], kv_sem.at[1]),
+        pltpu.make_async_copy(
+            other_ref.at[:, pl.ds(0, rows), :], kv.at[pl.ds(Y_SIZE, Y_SIZE)], kv_sem.at[1]),
     ]
     for copy in copies:
         copy.start()
@@ -94,10 +95,13 @@
             absorb(t, scores)
             scores = following
 
-    @pl.loop(0, PEERS)
-    def _(s):
-        query_x = lax.div(s, CORES)
-        query_core = lax.rem(s, CORES)
+    @pl.loop(0, CORES if own else PEERS - CORES)
+    def _(i):
+        turn = lax.div(i, CORES) + (0 if own else 1)
+        query_x = lax.rem(x + turn, X_SIZE)
+        query_core = lax.rem(i + core, CORES)
+        s = query_x * CORES + query_core
+        slot = i if own else s
         query_at = place_ref[ctx_of(query_x, y, query_core)]
 
         def note(i, found):
@@ -111,8 +115,7 @@
         total[...] = jnp.zeros_like(total)
         acc[...] = jnp.zeros_like(acc)
 
-        @pl.when(query_x == x)
-        def _():
+        if own:
             step(s, [jnp.where(query_core == core, y, Y_SIZE + y)], True)
 
         fours = lax.div(found, 4)
@@ -136,62 +139,70 @@
         for t in range(heads):
             lanes = slice(t * rows, (t + 1) * rows)
             norm = jnp.maximum(total[0:1, lanes], 1e-30)
-            out_ref[s, t * features:(t + 1) * features, :] = (
+            out_ref[slot, t * features:(t + 1) * features, :] = (
                 acc[:, lanes] * (1.0 / norm)).astype(jnp.bfloat16)
             left = top[0:1, lanes] * FACTOR + jnp.log(norm) * LOG2_E
             for part in range(3):
                 piece = left.astype(jnp.bfloat16).astype(jnp.float32)
                 stats = jnp.where(row == 3 * t + part, piece, stats)
                 left = left - piece
-        out_ref[s, heads * features:heads * features + STAT_ROWS, :] = stats.astype(jnp.bfloat16)
-
-
-def merge_kernel(heads, groups, part_ref, weight_ref, out_ref, hidden, weight, sems):
+        out_ref[slot, heads * features:heads * features + STAT_ROWS, :] = stats.astype(jnp.bfloat16)
+
+
+def merge_kernel(heads, groups, part_ref, own_ref, mate_ref, weight_ref, out_ref,
+                 hidden, chip, weight, sems):
     features = HEAD_FEATURES
     width = 2 * features
+    me = lax.axis_index("ctx")
+    core = lax.rem(me, CORES)
+    x = lax.div(me, CORES * Y_SIZE)
     copies = [
-        pltpu.make_async_copy(
-            weight_ref.at[x * CORES + c], weight.at[x, :, c], sems.at[x * CORES + c])
-        for x in range(X_SIZE) for c in range(CORES)
+        pltpu.make_async_copy(weight_ref.at[j], weight.at[j], sems.at[j]) for j in range(PEERS)
     ]
     for copy in copies:
         copy.start()
-
-    stats = [
-        part_ref[j, heads * features:heads * features + STAT_ROWS, :].astype(jnp.float32)
-        for j in range(PEERS)
-    ]
+    chip[core] = own_ref[0]
+    chip[1 - core] = mate_ref[0]
+
     for c in range(CORES):
+        sources = [chip.at[c]] + [
+            part_ref.at[lax.rem(x + turn, X_SIZE) * CORES + c] for turn in range(1, X_SIZE)
+        ]
+        stats = [
+            source[heads * features:heads * features + STAT_ROWS, :].astype(jnp.float32)
+            for source in sources
+        ]
         for t in range(heads):
-            peers = [i * CORES + c for i in range(X_SIZE)]
             levels = [
-                stats[j][3 * t:3 * t + 1] + stats[j][3 * t + 1:3 * t + 2]
-                + stats[j][3 * t + 2:3 * t + 3]
-                for j in peers
+                stat[3 * t:3 * t + 1] + stat[3 * t + 1:3 * t + 2] + stat[3 * t + 2:3 * t + 3]
+                for stat in stats
             ]
             peak = functools.reduce(jnp.maximum, levels)
             shares = [jnp.exp2(level - peak) for level in levels]
             inverse = 1.0 / sum(shares)
             merged = sum(
-                part_ref[j, t * features:(t + 1) * features, :].astype(jnp.float32)
+                source[t * features:(t + 1) * features, :].astype(jnp.float32)
                 * (share * inverse)
-                for j, share in zip(peers, shares)
+                for source, share in zip(sources, shares)
             )
             at = (c * heads + t) * features
             hidden[:, at:at + features] = merged.T.astype(jnp.bfloat16)
 
-    for copy in copies:
-        copy.wait()
     lines = X_SIZE * Y_SIZE // groups
     parts = Y_SIZE // lines
-    part_rows = weight.shape[3] // 2
+    part_rows = weight.shape[2] // 2
     for g in range(groups):
+        if g % parts == 0:
+            for c in range(CORES):
+                copies[(g // parts) * CORES + c].wait()
         term = None
         for side in range(2):
             start = (g % parts) * lines
-            piece = weight[g // parts, start:start + lines, :,
-                           side * part_rows:(side + 1) * part_rows, :].reshape(
-                lines * CORES * part_rows, width)
+            piece = jnp.concatenate([
+                weight[(g // parts) * CORES + c, start + line,
+                           side * part_rows:(side + 1) * part_rows, :]
+                for line in range(lines) for c in range(CORES)
+            ], 0)
             product = lax.dot_general(
                 hidden[:, side * width:(side + 1) * width], piece,
                 (((1,), (1,)), ((), ())), preferred_element_type=jnp.float32,
@@ -232,54 +243,60 @@
     asked = jnp.broadcast_to(asked[None], (X_SIZE,) + asked.shape).reshape(PEERS, rows, width)
     asked = lax.all_to_all(asked, "ctx", 0, 0, tiled=True, axis_index_groups=XC_GROUPS)
     asked = hold(asked)
-    other = lax.ppermute(line[:, :rows], "ctx", [(i, i ^ 1) for i in range(blocks)])
-    weights = lax.all_gather(line[:, rows:], "ctx", axis=0, axis_index_groups=XC_GROUPS)
-
-    parts = pl.pallas_call(
-        functools.partial(attend_kernel, rows, heads),
-        out_shape=jax.ShapeDtypeStruct((PEERS, width + STAT_ROWS, rows), jnp.bfloat16),
-        in_specs=[
-            pl.BlockSpec(memory_space=pltpu.SMEM),
-            pl.BlockSpec(memory_space=pltpu.VMEM),
-            pl.BlockSpec(memory_space=pl.ANY),
-            pl.BlockSpec(memory_space=pl.ANY),
-        ],
-        out_specs=pl.BlockSpec(memory_space=pltpu.VMEM),
-        scratch_shapes=[
-            pltpu.SMEM((SLOTS + 1,), jnp.int32),
-            pltpu.VMEM((SLOTS, rows, width), jnp.bfloat16),
-            pltpu.VMEM((8, heads * rows), jnp.float32),
-            pltpu.VMEM((8, heads * rows), jnp.float32),
-            pltpu.VMEM((HEAD_FEATURES, heads * rows), jnp.float32),
-            pltpu.SemaphoreType.DMA((2,)),
-        ],
-        compiler_params=pltpu.CompilerParams(
-            vmem_limit_bytes=32 * 1024 * 1024),
-        cost_estimate=pl.CostEstimate(
-            flops=9_000_000_000, transcendentals=9_000_000, bytes_accessed=5_000_000),
-        name="attend",
-    )(placement, asked, line, other)
-
+    swap = [(i, i ^ 1) for i in range(blocks)]
+    other = lax.ppermute(line, "ctx", swap)
+    spread = line[:, rows:]
+    weights = lax.all_gather(spread, "ctx", axis=0, axis_index_groups=XC_GROUPS)
+
+    def attend(own):
+        count = CORES if own else PEERS
+        return pl.pallas_call(
+            functools.partial(attend_kernel, own, rows, heads),
+            out_shape=jax.ShapeDtypeStruct((count, width + STAT_ROWS, rows), jnp.bfloat16),
+            in_specs=[
+                pl.BlockSpec(memory_space=pltpu.SMEM),
+                pl.BlockSpec(memory_space=pltpu.VMEM),
+                pl.BlockSpec(memory_space=pl.ANY),
+                pl.BlockSpec(memory_space=pl.ANY),
+            ],
+            out_specs=pl.BlockSpec(memory_space=pltpu.VMEM),
+            scratch_shapes=[
+                pltpu.SMEM((SLOTS + 1,), jnp.int32),
+                pltpu.VMEM((SLOTS, rows, width), jnp.bfloat16),
+                pltpu.VMEM((8, heads * rows), jnp.float32),
+                pltpu.VMEM((8, heads * rows), jnp.float32),
+                pltpu.VMEM((HEAD_FEATURES, heads * rows), jnp.float32),
+                pltpu.SemaphoreType.DMA((2,)),
+            ],
+            compiler_params=pltpu.CompilerParams(
+                vmem_limit_bytes=32 * 1024 * 1024),
+            cost_estimate=pl.CostEstimate(
+                flops=1_000_000_000 * count, transcendentals=1_000_000 * count,
+                bytes_accessed=5_000_000),
+        )(placement, asked, line, other)
+
+    parts = attend(False)
     gathered = lax.all_to_all(parts, "ctx", 0, 0, tiled=True, axis_index_groups=XC_GROUPS)
+    near = attend(True)
+    mate = lax.ppermute(near[1:], "ctx", swap)
 
     out_columns = blocks * turned.shape[0] // groups
-    weight_shape = (X_SIZE, Y_SIZE, CORES) + (2 * turned.shape[0], width)
     terms = pl.pallas_call(
         functools.partial(merge_kernel, heads, groups),
         out_shape=jax.ShapeDtypeStruct((groups, rows, out_columns), jnp.bfloat16),
         in_specs=[
             pl.BlockSpec(memory_space=pltpu.VMEM),
-            pl.BlockSpec(memory_space=pl.ANY),
-        ],
+        ] * 3 + [pl.BlockSpec(memory_space=pl.ANY)],
         out_specs=pl.BlockSpec(memory_space=pltpu.VMEM),
         scratch_shapes=[
             pltpu.VMEM((rows, columns), jnp.bfloat16),
-            pltpu.VMEM(weight_shape, jnp.bfloat16),
+            pltpu.VMEM((CORES, width + STAT_ROWS, rows), jnp.bfloat16),
+            pltpu.VMEM(weights.shape, jnp.bfloat16),
             pltpu.SemaphoreType.DMA((PEERS,)),
         ],
-        compiler_params=pltpu.CompilerParams(vmem_limit_bytes=32 * 1024 * 1024),
+        compiler_params=pltpu.CompilerParams(vmem_limit_bytes=60 * 1024 * 1024),
         name="merge_project",
-    )(gathered, weights)
+    )(gathered, near, mate, weights)
     return lax.psum_scatter(
         terms.reshape(groups * rows, out_columns), "head", scatter_dimension=0, tiled=True
     )

time: 187 us -> 183 us (0.979)
  the two profiles are of different devices: /device:TPU:10 before, /device:TPU:16 now
where the time goes in v4:
time: 183 us; the launch traced here: 182 us
  waiting for transfers between devices  96.2 us (53%)
  Pallas kernels  37.1 us (20%)
  blocking collectives  23.6 us (13%)
  between operations  13.2 us (7%)
  starting transfers between devices  8.84 us (5%)
  local copies, waits for them, and re-layouts  3.35 us (2%)
    all_gather x1, waiting for transfers between devices, body(): line = lax.all_gather(sent, 'ctx', axis=0, axis_index_groups=Y_GROUPS)  46.4 us
    reduce_scatter x1, waiting for transfers between devices, body(): lax.psum_scatter(terms.reshape(groups * rows, out_columns), 'head', scatt...  43.6 us
    pallas_call x2, Pallas kernels, attend(): pl.pallas_call(functools.partial(attend_kernel, own, rows, heads), out_sh...  29.5 us
    all_to_all x1, blocking collectives, body(): lax.all_to_all(asked, 'ctx', 0, 0, tiled=True, axis_index_groups=XC_GROUPS)  23.6 us
    pallas_call x1, Pallas kernels, body(): pl.pallas_call(functools.partial(merge_kernel, heads, groups), out_shape=...  5.88 us
    all_to_all x1, waiting for transfers between devices, body(): lax.all_to_all(parts, 'ctx', 0, 0, tiled=True, axis_index_groups=XC_GROUPS)  5.15 us
    all_to_all x1, starting transfers between devices, body(): lax.all_to_all(parts, 'ctx', 0, 0, tiled=True, axis_index_groups=XC_GROUPS)  4.47 us
  transfers between devices with their start and end apart: 6, of which 4 were waited for; matrix products, arithmetic and copies ran while one was open for 0% of the time, Pallas kernels for 16%

profile of v4, /device:TPU:16, one launch (start us, length us, event | category | flops | bytes accessed | tf_op | source)
XLA Modules:
  0.0 182.4 jit_solution(10152556436301413190)
XLA Ops:
  6.5 0.0 copy-start.5
  6.5 0.0 all-gather.5.cloned.1.call-start
  6.5 1.7 pack.1
  8.3 0.0 all-gather.5.cloned.1.call-update
  8.3 0.0 all-gather.7.cloned.1.call-start
  8.3 46.4 %all-gather.5.cloned.1.call-done = bf16[3072,256]{1,0:T(8,128)(2,1)} async-done(((bf16[384,256]{1,0:T(8,128)(2,1)}), bf16[3072,256]{1,0:T(8,128)(2,1)}) %all-gather.5.cloned.1.call-update) | async-done | bytes 1572880 | tf_op jit(solution)/shard_map/all_gather | solution.py:240
  54.7 0.0 copy-start.3
  54.7 2.0 %slice.17 = bf16[8,128,256]{2,1,0:T(8,128)(2,1)} slice(bf16[8,384,256]{2,1,0:T(8,128)(2,1)} %bitcast.9), slice={[0:8], [256:384], [0:256]} | slice | bytes 1048576 | tf_op jit(solution)/shard_map/slice | solution.py:248
  56.7 0.0 all-gather.7.cloned.1.call-update
  56.8 0.0 copy-done.3
  56.8 1.9 %collective-permute-start = (bf16[8,384,256]{2,1,0:T(8,128)(2,1)S(1)}, bf16[8,384,256]{2,1,0:T(8,128)(2,1)}, u32[]{:S(2)}, u32[]{:S(2)}) collective-permute-start(bf16[8,384,256]{2,1,0:T(8,128)(2,1)S(1)} %bitcast.10), channel_id=1, source_target_pairs={{0,8},{8,0},{16,24},{24,16},{32,40},{40,32},{48,56},{56,48},{64,72... | collective-permute-start | bytes 4718600 | tf_op jit(solution)/shard_map/ppermute | solution.py:247
  58.7 0.0 copy-done.5
  58.8 0.1 broadcast_in_dim.2
  58.9 0.0 copy-start.4
  58.9 23.6 %all_to_all.10.array_ref = bf16[8,256,256]{2,1,0:T(8,128)(2,1)} all-to-all(bf16[8,256,256]{2,1,0:T(8,128)(2,1)S(1)} %bitcast.14), channel_id=1, replica_groups={{0,8,128,136,256,264,384,392},{16,24,144,152,272,280,400,408},{32,40,16..., dimensions={0} | all-to-all | bytes 2097152 | tf_op jit(solution)/shard_map/all_to_all | solution.py:244
  82.5 0.0 collective-permute-done.other_ref
  82.5 0.0 copy-done.4
  82.5 0.0 copy-start
  82.5 1.2 copy-done
  83.7 21.4 %shard_map.55 = bf16[8,272,256]{2,1,0:T(8,128)(2,1)} custom-call(s32[64]{0:T(128)S(1)} %copy-done.4, bf16[8,256,256]{2,1,0:T(8,128)(2,1)S(1)} %copy-done, bf16[8,384,256]{2,1,0:T(8,128)(2,1)S(1)} %bitcast.11, bf16[8,384,256]{2,1,0:T(8,128)(2,1)} %collective-permute-done.other_ref), custom_call_target="tpu_custom_call" | custom-call | flops 8000000000 | bytes 5000000 | tf_op jit(solution)/shard_map/pallas_call | solution.py:253
  105.1 0.0 copy-start.1
  105.1 4.5 %all-to-all-start.1 = ((bf16[8,272,256]{2,1,0:T(8,128)(2,1)}), bf16[8,272,256]{2,1,0:T(8,128)(2,1)}, u32[]{:S(2)}, u32[]{:S(2)}) async-start(bf16[8,272,256]{2,1,0:T(8,128)(2,1)} %shard_map.55), calls=%async_computation.1 | async-start | bytes 2228224 | tf_op jit(solution)/shard_map/all_to_all | solution.py:279
  109.6 0.0 reduce-scatter.2.cloned.1.call-start
  109.6 0.0 copy-done.1
  109.6 8.1 %shard_map.56.own_ref = bf16[2,272,256]{2,1,0:T(8,128)(2,1)S(1)} custom-call(s32[64]{0:T(128)S(1)} %copy-done.4, bf16[8,256,256]{2,1,0:T(8,128)(2,1)S(1)} %copy-done.1, bf16[8,384,256]{2,1,0:T(8,128)(2,1)S(1)} %bitcast.12, bf16[8,384,256]{2,1,0:T(8,128)(2,1)} %collective-permute-done.other_ref), custom_call_target="tpu_custom_call" | custom-call | flops 2000000000 | bytes 5000000 | tf_op jit(solution)/shard_map/pallas_call | solution.py:253
  117.8 0.0 copy-start.2
  117.8 2.4 %collective-permute-start.1 = (bf16[1,272,256]{2,1,0:T(8,128)(2,1)S(1)}, bf16[1,272,256]{2,1,0:T(8,128)(2,1)S(1)}, u32[]{:S(2)}, u32[]{:S(2)}) collective-permute-start(bf16[1,272,256]{2,1,0:T(8,128)(2,1)S(1)} %slice.16), channel_id=1, source_target_pairs={{0,8},{8,0},{16,24},{24,16},{32,40},{40,32},{48,56},{56,48},{64,72... | collective-permute-start | bytes 417800 | tf_op jit(solution)/shard_map/ppermute | solution.py:281
  120.2 1.0 collective-permute-done.1.mate_ref
  121.2 0.0 copy-start.6
  121.2 5.1 %all-to-all-done.1.part_ref = bf16[8,272,256]{2,1,0:T(8,128)(2,1)} async-done(((bf16[8,272,256]{2,1,0:T(8,128)(2,1)}), bf16[8,272,256]{2,1,0:T(8,128)(2,1)}, u32[]{:S(2)}, u32[]{:S(2)}) %all-to-all-start.1) | async-done | bytes 1114144 | tf_op jit(solution)/shard_map/all_to_all | solution.py:279
  126.3 0.0 all-gather.7.cloned.1.call-done
  126.3 0.0 copy-done.2
  126.3 0.0 copy-done.6
  126.3 5.9 %merge_project.1 = bf16[8,256,512]{2,1,0:T(8,128)(2,1)} custom-call(bf16[8,272,256]{2,1,0:T(8,128)(2,1)} %all-to-all-done.1.part_ref, bf16[2,272,256]{2,1,0:T(8,128)(2,1)} %copy-done.2, bf16[1,272,256]{2,1,0:T(8,128)(2,1)} %copy-done.6, bf16[8,8,128,256]{3,2,1,0:T(8,128)(2,1)} %bitcast.15), custom_call_target="tpu_custom_call" | custom-call | tf_op jit(solution)/shard_map/merge_project/pallas_call | solution.py:284
  132.2 0.0 reduce-scatter.2.cloned.1.call-update
  132.2 43.6 %reduce-scatter.2.cloned.1.call-done = bf16[256,512]{1,0:T(8,128)(2,1)} async-done(((bf16[2048,512]{1,0:T(8,128)(2,1)}), bf16[256,512]{1,0:T(8,128)(2,1)}) %reduce-scatter.2.cloned.1.call-update) | async-done | bytes 262160 | tf_op jit(solution)/shard_map/reduce_scatter | solution.py:300
  (4 shorter events, 0.1 us)
Async XLA Ops:
  6.5 52.2 %copy-start.5 = (bf16[256,512]{1,0:T(8,128)(2,1)S(1)}, bf16[256,512]{1,0:T(8,128)(2,1)}, u32[]{:S(2)}) copy-start(bf16[256,512]{1,0:T(8,128)(2,1)} %param.6) | copy-start | bytes 786436
  6.5 48.2 %all-gather.5.cloned.1.call-start = ((), (), s32[]{:S(2)}) async-start(), calls=%async_computation.4 | async-start | bytes 1769472 | tf_op jit(solution)/shard_map/all_gather | solution.py:240
  8.3 118.0 %all-gather.7.cloned.1.call-start = ((), (), s32[]{:S(2)}) async-start(), calls=%async_computation.5 | async-start | bytes 4718592 | tf_op jit(solution)/shard_map/all_gather | solution.py:249
  54.7 2.0 %copy-start.3 = (bf16[3072,256]{1,0:T(8,128)(2,1)S(1)}, bf16[3072,256]{1,0:T(8,128)(2,1)}, u32[]{:S(2)}) copy-start(bf16[3072,256]{1,0:T(8,128)(2,1)} %all-gather.5.cloned.1.call-done) | copy-start | bytes 4718596
  56.8 25.7 %collective-permute-start = (bf16[8,384,256]{2,1,0:T(8,128)(2,1)S(1)}, bf16[8,384,256]{2,1,0:T(8,128)(2,1)}, u32[]{:S(2)}, u32[]{:S(2)}) collective-permute-start(bf16[8,384,256]{2,1,0:T(8,128)(2,1)S(1)} %bitcast.10), channel_id=1, source_target_pairs={{0,8},{8,0},{16,24},{24,16},{32,40},{40,32},{48,56},{56,48},{64,72... | collective-permute-start | bytes 4718600 | tf_op jit(solution)/shard_map/ppermute | solution.py:247
  58.9 23.6 %copy-start.4 = (s32[64]{0:T(128)S(1)}, s32[64]{0:T(128)}, u32[]{:S(2)}) copy-start(s32[64]{0:T(128)} %place_ref.3) | copy-start | bytes 772
  82.5 1.2 copy-start
  105.1 4.5 %copy-start.1 = (bf16[8,256,256]{2,1,0:T(8,128)(2,1)S(1)}, bf16[8,256,256]{2,1,0:T(8,128)(2,1)}, u32[]{:S(2)}) copy-start(bf16[8,256,256]{2,1,0:T(8,128)(2,1)} %hold.1.q_ref) | copy-start | bytes 3145732
  105.1 21.2 %all-to-all-start.1 = ((bf16[8,272,256]{2,1,0:T(8,128)(2,1)}), bf16[8,272,256]{2,1,0:T(8,128)(2,1)}, u32[]{:S(2)}, u32[]{:S(2)}) async-start(bf16[8,272,256]{2,1,0:T(8,128)(2,1)} %shard_map.55), calls=%async_computation.1 | async-start | bytes 2228224 | tf_op jit(solution)/shard_map/all_to_all | solution.py:279
  109.6 66.3 %reduce-scatter.2.cloned.1.call-start = ((), (), s32[]{:S(2)}) async-start(), calls=%async_computation.3 | async-start | bytes 2359296 | tf_op jit(solution)/shard_map/reduce_scatter | solution.py:300
  117.8 8.5 %copy-start.2 = (bf16[2,272,256]{2,1,0:T(8,128)(2,1)}, bf16[2,272,256]{2,1,0:T(8,128)(2,1)S(1)}, u32[]{:S(2)}) copy-start(bf16[2,272,256]{2,1,0:T(8,128)(2,1)S(1)} %shard_map.56.own_ref) | copy-start | bytes 835588
  117.8 3.4 %collective-permute-start.1 = (bf16[1,272,256]{2,1,0:T(8,128)(2,1)S(1)}, bf16[1,272,256]{2,1,0:T(8,128)(2,1)S(1)}, u32[]{:S(2)}, u32[]{:S(2)}) collective-permute-start(bf16[1,272,256]{2,1,0:T(8,128)(2,1)S(1)} %slice.16), channel_id=1, source_target_pairs={{0,8},{8,0},{16,24},{24,16},{32,40},{40,32},{48,56},{56,48},{64,72... | collective-permute-start | bytes 417800 | tf_op jit(solution)/shard_map/ppermute | solution.py:281
  121.2 5.2 %copy-start.6 = (bf16[1,272,256]{2,1,0:T(8,128)(2,1)}, bf16[1,272,256]{2,1,0:T(8,128)(2,1)S(1)}, u32[]{:S(2)}) copy-start(bf16[1,272,256]{2,1,0:T(8,128)(2,1)S(1)} %collective-permute-done.1.mate_ref) | copy-start | bytes 417796
Sparse Core Ops, SparseCore 0:
  9.4 45.2 all-gather.4
  56.9 40.2 all-gather.6
  132.4 43.4 reduce-scatter.1

commit v5 on v4

--- a/solution.py
+++ b/solution.py
@@ -38,8 +38,7 @@
             weight_ref[:, i * width:(i + 1) * width])
 
 
-def attend_kernel(own, rows, heads, place_ref, q_ref, line_ref, other_ref, out_ref,
-                  listed, kv, top, total, acc, kv_sem):
+def attend_kernel(own, rows, heads, place_ref, ask_ref, *refs):
     features = HEAD_FEATURES
     half = rows // 2
     me = lax.axis_index("ctx")
@@ -47,16 +46,25 @@
     y = lax.rem(lax.div(me, CORES), Y_SIZE)
     x = lax.div(me, CORES * Y_SIZE)
 
-    copies = [
-        pltpu.make_async_copy(
-            line_ref.at[:, pl.ds(0, rows), :], kv.at[pl.ds(0, Y_SIZE)], kv_sem.at[0]),
-        pltpu.make_async_copy(
-            other_ref.at[:, pl.ds(0, rows), :], kv.at[pl.ds(Y_SIZE, Y_SIZE)], kv_sem.at[1]),
-    ]
+    if own:
+        kept_ref, out_ref, listed, q_ref, kv, top, total, acc, kv_sem = refs
+        copies = [pltpu.make_async_copy(kept_ref, kv, kv_sem.at[0])]
+    else:
+        line_ref, other_ref, out_ref, kept_ref, listed, q_ref, kv, top, total, acc, kv_sem = refs
+        copies = [
+            pltpu.make_async_copy(
+                line_ref.at[:, pl.ds(0, rows), :], kv.at[pl.ds(0, Y_SIZE)], kv_sem.at[0]),
+            pltpu.make_async_copy(
+                other_ref.at[:, pl.ds(0, rows), :], kv.at[pl.ds(Y_SIZE, Y_SIZE)], kv_sem.at[1]),
+        ]
+    copies.append(pltpu.make_async_copy(ask_ref, q_ref, kv_sem.at[2]))
     for copy in copies:
         copy.start()
     for copy in copies:
         copy.wait()
+    if not own:
+        keep = pltpu.make_async_copy(kv, kept_ref, kv_sem.at[3])
+        keep.start()
 
     def step(s, slots, masked):
         keys = jnp.concatenate(
@@ -147,6 +155,9 @@
                 stats = jnp.where(row == 3 * t + part, piece, stats)
                 left = left - piece
         out_ref[slot, heads * features:heads * features + STAT_ROWS, :] = stats.astype(jnp.bfloat16)
+
+    if not own:
+        keep.wait()
 
 
 def merge_kernel(heads, groups, part_ref, own_ref, mate_ref, weight_ref, out_ref,
@@ -243,41 +254,49 @@
     asked = jnp.broadcast_to(asked[None], (X_SIZE,) + asked.shape).reshape(PEERS, rows, width)
     asked = lax.all_to_all(asked, "ctx", 0, 0, tiled=True, axis_index_groups=XC_GROUPS)
     asked = hold(asked)
+    asked = pltpu.with_memory_space_constraint(asked, pltpu.HBM)
     swap = [(i, i ^ 1) for i in range(blocks)]
     other = lax.ppermute(line, "ctx", swap)
+    held = pltpu.with_memory_space_constraint(line, pltpu.HBM)
     spread = line[:, rows:]
     weights = lax.all_gather(spread, "ctx", axis=0, axis_index_groups=XC_GROUPS)
-
-    def attend(own):
+    weights = pltpu.with_memory_space_constraint(weights, pltpu.HBM)
+
+    def attend(own, *lines):
         count = CORES if own else PEERS
+        out_shape = [jax.ShapeDtypeStruct((count, width + STAT_ROWS, rows), jnp.bfloat16)]
+        out_specs = [pl.BlockSpec(memory_space=pltpu.VMEM)]
+        if not own:
+            out_shape.append(jax.ShapeDtypeStruct((SLOTS, rows, width), jnp.bfloat16))
+            out_specs.append(pl.BlockSpec(memory_space=pltpu.HBM))
         return pl.pallas_call(
             functools.partial(attend_kernel, own, rows, heads),
-            out_shape=jax.ShapeDtypeStruct((count, width + STAT_ROWS, rows), jnp.bfloat16),
+            out_shape=out_shape,
             in_specs=[
                 pl.BlockSpec(memory_space=pltpu.SMEM),
-                pl.BlockSpec(memory_space=pltpu.VMEM),
-                pl.BlockSpec(memory_space=pl.ANY),
-                pl.BlockSpec(memory_space=pl.ANY),
-            ],
-            out_specs=pl.BlockSpec(memory_space=pltpu.VMEM),
+                pl.BlockSpec(memory_space=pltpu.HBM),
+            ] + [pl.BlockSpec(memory_space=pl.ANY)] * len(lines),
+            out_specs=out_specs,
             scratch_shapes=[
                 pltpu.SMEM((SLOTS + 1,), jnp.int32),
+                pltpu.VMEM((PEERS, rows, width), jnp.bfloat16),
                 pltpu.VMEM((SLOTS, rows, width), jnp.bfloat16),
                 pltpu.VMEM((8, heads * rows), jnp.float32),
                 pltpu.VMEM((8, heads * rows), jnp.float32),
                 pltpu.VMEM((HEAD_FEATURES, heads * rows), jnp.float32),
-                pltpu.SemaphoreType.DMA((2,)),
+                pltpu.SemaphoreType.DMA((4,)),
             ],
             compiler_params=pltpu.CompilerParams(
-                vmem_limit_bytes=32 * 1024 * 1024),
+                vmem_limit_bytes=(32 << 20) if own else 62900000),
             cost_estimate=pl.CostEstimate(
                 flops=1_000_000_000 * count, transcendentals=1_000_000 * count,
                 bytes_accessed=5_000_000),
-        )(placement, asked, line, other)
-
-    parts = attend(False)
+        )(placement, asked, *lines)
+
+    parts, kept = attend(False, held, other)
+    kept = pltpu.with_memory_space_constraint(kept, pltpu.HBM)
     gathered = lax.all_to_all(parts, "ctx", 0, 0, tiled=True, axis_index_groups=XC_GROUPS)
-    near = attend(True)
+    near, = attend(True, kept)
     mate = lax.ppermute(near[1:], "ctx", swap)
 
     out_columns = blocks * turned.shape[0] // groups
@@ -286,7 +305,7 @@
         out_shape=jax.ShapeDtypeStruct((groups, rows, out_columns), jnp.bfloat16),
         in_specs=[
             pl.BlockSpec(memory_space=pltpu.VMEM),
-        ] * 3 + [pl.BlockSpec(memory_space=pl.ANY)],
+        ] * 3 + [pl.BlockSpec(memory_space=pltpu.HBM)],
         out_specs=pl.BlockSpec(memory_space=pltpu.VMEM),
         scratch_shapes=[
             pltpu.VMEM((rows, columns), jnp.bfloat16),
@@ -294,7 +313,7 @@
             pltpu.VMEM(weights.shape, jnp.bfloat16),
             pltpu.SemaphoreType.DMA((PEERS,)),
         ],
-        compiler_params=pltpu.CompilerParams(vmem_limit_bytes=60 * 1024 * 1024),
+        compiler_params=pltpu.CompilerParams(vmem_limit_bytes=32 * 1024 * 1024),
         name="merge_project",
     )(gathered, near, mate, weights)
     return lax.psum_scatter(

time: 183 us -> 181 us (0.989)
  the two profiles are of different devices: /device:TPU:16 before, /device:TPU:8 now
where the time goes in v5:
time: 181 us
  waiting for transfers between devices  95.6 us (53%)
  Pallas kernels  36.4 us (20%)
  blocking collectives  24.4 us (13%)
  between operations  13.2 us (7%)
  starting transfers between devices  7.84 us (4%)
  local copies, waits for them, and re-layouts  3.34 us (2%)
    all_gather x1, waiting for transfers between devices, body(): line = lax.all_gather(sent, 'ctx', axis=0, axis_index_groups=Y_GROUPS)  47.4 us
    reduce_scatter x1, waiting for transfers between devices, body(): lax.psum_scatter(terms.reshape(groups * rows, out_columns), 'head', scatt...  42.4 us
    pallas_call x2, Pallas kernels, attend(): pl.pallas_call(functools.partial(attend_kernel, own, rows, heads), out_sh...  29.9 us
    all_to_all x1, blocking collectives, body(): lax.all_to_all(asked, 'ctx', 0, 0, tiled=True, axis_index_groups=XC_GROUPS)  24.4 us
    all_to_all x1, waiting for transfers between devices, body(): lax.all_to_all(parts, 'ctx', 0, 0, tiled=True, axis_index_groups=XC_GROUPS)  4.81 us
    pallas_call x1, Pallas kernels, body(): pl.pallas_call(functools.partial(merge_kernel, heads, groups), out_shape=...  4.77 us
  transfers between devices with their start and end apart: 6, of which 4 were waited for; matrix products, arithmetic and copies ran while one was open for 0% of the time, Pallas kernels for 17%

profile of v5, /device:TPU:8, one launch (start us, length us, event | category | flops | bytes accessed | tf_op | source)
XLA Modules:
  0.0 180.9 jit_solution(11093658423922380497)
XLA Ops:
  6.5 0.0 copy-start.1
  6.5 0.0 all-gather.5.cloned.1.call-start
  6.5 1.7 pack.1
  8.3 0.0 all-gather.5.cloned.1.call-update
  8.3 0.0 all-gather.7.cloned.1.call-start
  8.3 47.4 %all-gather.5.cloned.1.call-done = bf16[3072,256]{1,0:T(8,128)(2,1)} async-done(((bf16[384,256]{1,0:T(8,128)(2,1)}), bf16[3072,256]{1,0:T(8,128)(2,1)}) %all-gather.5.cloned.1.call-update) | async-done | bytes 1572880 | tf_op jit(solution)/shard_map/all_gather | solution.py:251
  55.7 0.0 copy-start.2
  55.7 2.0 %slice.17 = bf16[8,128,256]{2,1,0:T(8,128)(2,1)} slice(bf16[8,384,256]{2,1,0:T(8,128)(2,1)} %bitcast.11), slice={[0:8], [256:384], [0:256]} | slice | bytes 1048576 | tf_op jit(solution)/shard_map/slice | solution.py:261
  57.7 0.0 all-gather.7.cloned.1.call-update
  57.7 0.0 copy-done.2
  57.7 1.9 %collective-permute-start = (bf16[8,384,256]{2,1,0:T(8,128)(2,1)S(1)}, bf16[8,384,256]{2,1,0:T(8,128)(2,1)S(1)}, u32[]{:S(2)}, u32[]{:S(2)}) collective-permute-start(bf16[8,384,256]{2,1,0:T(8,128)(2,1)S(1)} %bitcast.13), channel_id=1, source_target_pairs={{0,8},{8,0},{16,24},{24,16},{32,40},{40,32},{48,56},{56,48},{64,72... | collective-permute-start | bytes 4718600 | tf_op jit(solution)/shard_map/ppermute | solution.py:259
  59.7 0.0 copy-done.1
  59.7 0.1 broadcast_in_dim.2
  59.8 24.4 %all_to_all.10.array_ref = bf16[8,256,256]{2,1,0:T(8,128)(2,1)} all-to-all(bf16[8,256,256]{2,1,0:T(8,128)(2,1)S(1)} %bitcast.9), channel_id=1, replica_groups={{0,8,128,136,256,264,384,392},{16,24,144,152,272,280,400,408},{32,40,16..., dimensions={0} | all-to-all | bytes 2097152 | tf_op jit(solution)/shard_map/all_to_all | solution.py:255
  84.3 0.0 collective-permute-done.refs_1_
  84.3 0.0 copy-start.3
  84.3 1.2 copy-done.3
  85.5 21.5 %shard_map.55 = (bf16[8,272,256]{2,1,0:T(8,128)(2,1)}, bf16[16,256,256]{2,1,0:T(8,128)(2,1)}) custom-call(s32[64]{0:T(128)} %place_ref.3, bf16[8,256,256]{2,1,0:T(8,128)(2,1)} %hold.1.ask_ref, bf16[8,384,256]{2,1,0:T(8,128)(2,1)} %bitcast.12, bf16[8,384,256]{2,1,0:T(8,128)(2,1)} %copy-done.3), custom_call_target="tpu_custom_call" | custom-call | flops 8000000000 | bytes 5000000 | tf_op jit(solution)/shard_map/pallas_call | solution.py:272
  107.0 0.0 copy-start
  107.0 3.6 %all-to-all-start.1 = ((bf16[8,272,256]{2,1,0:T(8,128)(2,1)}), bf16[8,272,256]{2,1,0:T(8,128)(2,1)S(1)}, u32[]{:S(2)}, u32[]{:S(2)}) async-start(bf16[8,272,256]{2,1,0:T(8,128)(2,1)} %get-tuple-element.7), calls=%async_computation.1 | async-start | bytes 2228224 | tf_op jit(solution)/shard_map/all_to_all | solution.py:298
  110.6 0.0 reduce-scatter.2.cloned.1.call-start
  110.7 0.0 copy-done
  110.7 8.4 %shard_map.56.own_ref = bf16[2,272,256]{2,1,0:T(8,128)(2,1)S(1)} custom-call(s32[64]{0:T(128)S(1)} %copy-done, bf16[8,256,256]{2,1,0:T(8,128)(2,1)} %hold.1.ask_ref, bf16[16,256,256]{2,1,0:T(8,128)(2,1)} %get-tuple-element.8.refs_0_), custom_call_target="tpu_custom_call" | custom-call | flops 2000000000 | bytes 5000000 | tf_op jit(solution)/shard_map/pallas_call | solution.py:272
  119.1 2.3 %collective-permute-start.1 = (bf16[1,272,256]{2,1,0:T(8,128)(2,1)S(1)}, bf16[1,272,256]{2,1,0:T(8,128)(2,1)S(1)}, u32[]{:S(2)}, u32[]{:S(2)}) collective-permute-start(bf16[1,272,256]{2,1,0:T(8,128)(2,1)S(1)} %slice.16), channel_id=1, source_target_pairs={{0,8},{8,0},{16,24},{24,16},{32,40},{40,32},{48,56},{56,48},{64,72... | collective-permute-start | bytes 417800 | tf_op jit(solution)/shard_map/ppermute | solution.py:300
  121.4 1.0 collective-permute-done.1.mate_ref
  122.4 4.8 %all-to-all-done.1.part_ref = bf16[8,272,256]{2,1,0:T(8,128)(2,1)S(1)} async-done(((bf16[8,272,256]{2,1,0:T(8,128)(2,1)}), bf16[8,272,256]{2,1,0:T(8,128)(2,1)S(1)}, u32[]{:S(2)}, u32[]{:S(2)}) %all-to-all-start.1) | async-done | bytes 1114144 | tf_op jit(solution)/shard_map/all_to_all | solution.py:298
  127.2 0.0 all-gather.7.cloned.1.call-done
  127.2 4.8 %merge_project.1 = bf16[8,256,512]{2,1,0:T(8,128)(2,1)} custom-call(bf16[8,272,256]{2,1,0:T(8,128)(2,1)S(1)} %all-to-all-done.1.part_ref, bf16[2,272,256]{2,1,0:T(8,128)(2,1)S(1)} %shard_map.56.own_ref, bf16[1,272,256]{2,1,0:T(8,128)(2,1)S(1)} %collective-permute-done.1.mate_ref, bf16[8,8,128,256]{3,2,1,0:T(8,128)(2,1)} %bitcast.10), custom_call_target="tpu_custom_call" | custom-call | tf_op jit(solution)/shard_map/merge_project/pallas_call | solution.py:303
  132.0 0.0 reduce-scatter.2.cloned.1.call-update
  132.0 42.4 %reduce-scatter.2.cloned.1.call-done = bf16[256,512]{1,0:T(8,128)(2,1)} async-done(((bf16[2048,512]{1,0:T(8,128)(2,1)}), bf16[256,512]{1,0:T(8,128)(2,1)}) %reduce-scatter.2.cloned.1.call-update) | async-done | bytes 262160 | tf_op jit(solution)/shard_map/reduce_scatter | solution.py:319
  (4 shorter events, 0.1 us)
Async XLA Ops:
  6.5 53.1 %copy-start.1 = (bf16[256,512]{1,0:T(8,128)(2,1)S(1)}, bf16[256,512]{1,0:T(8,128)(2,1)}, u32[]{:S(2)}) copy-start(bf16[256,512]{1,0:T(8,128)(2,1)} %param.6) | copy-start | bytes 786436
  6.5 49.2 %all-gather.5.cloned.1.call-start = ((), (), s32[]{:S(2)}) async-start(), calls=%async_computation.4 | async-start | bytes 1769472 | tf_op jit(solution)/shard_map/all_gather | solution.py:251
  8.3 118.9 %all-gather.7.cloned.1.call-start = ((), (), s32[]{:S(2)}) async-start(), calls=%async_computation.5 | async-start | bytes 4718592 | tf_op jit(solution)/shard_map/all_gather | solution.py:262
  55.7 2.0 %copy-start.2 = (bf16[3072,256]{1,0:T(8,128)(2,1)S(1)}, bf16[3072,256]{1,0:T(8,128)(2,1)}, u32[]{:S(2)}) copy-start(bf16[3072,256]{1,0:T(8,128)(2,1)} %all-gather.5.cloned.1.call-done) | copy-start | bytes 4718596
  57.7 26.5 %collective-permute-start = (bf16[8,384,256]{2,1,0:T(8,128)(2,1)S(1)}, bf16[8,384,256]{2,1,0:T(8,128)(2,1)S(1)}, u32[]{:S(2)}, u32[]{:S(2)}) collective-permute-start(bf16[8,384,256]{2,1,0:T(8,128)(2,1)S(1)} %bitcast.13), channel_id=1, source_target_pairs={{0,8},{8,0},{16,24},{24,16},{32,40},{40,32},{48,56},{56,48},{64,72... | collective-permute-start | bytes 4718600 | tf_op jit(solution)/shard_map/ppermute | solution.py:259
  84.3 1.2 copy-start.3
  107.0 3.6 %copy-start = (s32[64]{0:T(128)S(1)}, s32[64]{0:T(128)}, u32[]{:S(2)}) copy-start(s32[64]{0:T(128)} %place_ref.3) | copy-start | bytes 772
  107.0 20.1 %all-to-all-start.1 = ((bf16[8,272,256]{2,1,0:T(8,128)(2,1)}), bf16[8,272,256]{2,1,0:T(8,128)(2,1)S(1)}, u32[]{:S(2)}, u32[]{:S(2)}) async-start(bf16[8,272,256]{2,1,0:T(8,128)(2,1)} %get-tuple-element.7), calls=%async_computation.1 | async-start | bytes 2228224 | tf_op jit(solution)/shard_map/all_to_all | solution.py:298
  110.6 63.8 %reduce-scatter.2.cloned.1.call-start = ((), (), s32[]{:S(2)}) async-start(), calls=%async_computation.3 | async-start | bytes 2359296 | tf_op jit(solution)/shard_map/reduce_scatter | solution.py:319
  119.1 3.3 %collective-permute-start.1 = (bf16[1,272,256]{2,1,0:T(8,128)(2,1)S(1)}, bf16[1,272,256]{2,1,0:T(8,128)(2,1)S(1)}, u32[]{:S(2)}, u32[]{:S(2)}) collective-permute-start(bf16[1,272,256]{2,1,0:T(8,128)(2,1)S(1)} %slice.16), channel_id=1, source_target_pairs={{0,8},{8,0},{16,24},{24,16},{32,40},{40,32},{48,56},{56,48},{64,72... | collective-permute-start | bytes 417800 | tf_op jit(solution)/shard_map/ppermute | solution.py:300
Sparse Core Ops, SparseCore 0:
  9.4 46.2 all-gather.4
  57.9 40.2 all-gather.6
  132.1 42.2 reduce-scatter.1

commit v6 on v5

--- a/solution.py
+++ b/solution.py
@@ -21,21 +21,18 @@
     return (x * Y_SIZE + y) * CORES + core
 
 
+X_GROUPS = [[ctx_of(x, y, c) for x in range(X_SIZE)] for y in range(Y_SIZE) for c in range(CORES)]
 Y_GROUPS = [[ctx_of(x, y, c) for y in range(Y_SIZE)] for x in range(X_SIZE) for c in range(CORES)]
 XC_GROUPS = [[ctx_of(x, y, c) for x in range(X_SIZE) for c in range(CORES)] for y in range(Y_SIZE)]
 
 
-def pack_kernel(key_ref, value_ref, weight_ref, out_ref):
+def pack_kernel(key_ref, value_ref, out_ref):
     rows, features = key_ref.shape
     half = rows // 2
-    count = weight_ref.shape[0]
     width = out_ref.shape[1]
     out_ref[0:half, 0:features] = key_ref[0:half, :]
     out_ref[0:half, features:width] = key_ref[half:rows, :]
     out_ref[half:rows, :] = value_ref[...].astype(jnp.float32).T.astype(jnp.bfloat16)
-    for i in range(2):
-        out_ref[rows + i * count:rows + (i + 1) * count, :] = (
-            weight_ref[:, i * width:(i + 1) * width])
 
 
 def attend_kernel(own, rows, heads, place_ref, ask_ref, *refs):
@@ -53,9 +50,9 @@
         line_ref, other_ref, out_ref, kept_ref, listed, q_ref, kv, top, total, acc, kv_sem = refs
         copies = [
             pltpu.make_async_copy(
-                line_ref.at[:, pl.ds(0, rows), :], kv.at[pl.ds(0, Y_SIZE)], kv_sem.at[0]),
+                line_ref, kv.at[pl.ds(0, Y_SIZE)], kv_sem.at[0]),
             pltpu.make_async_copy(
-                other_ref.at[:, pl.ds(0, rows), :], kv.at[pl.ds(Y_SIZE, Y_SIZE)], kv_sem.at[1]),
+                other_ref, kv.at[pl.ds(Y_SIZE, Y_SIZE)], kv_sem.at[1]),
         ]
     copies.append(pltpu.make_async_copy(ask_ref, q_ref, kv_sem.at[2]))
     for copy in copies:
@@ -112,13 +109,12 @@
         slot = i if own else s
         query_at = place_ref[ctx_of(query_x, y, query_core)]
 
-        def note(i, found):
-            slot_core = jnp.where(i < Y_SIZE, core, 1 - core)
-            key_at = place_ref[ctx_of(x, lax.rem(i, Y_SIZE), slot_core)]
-            listed[found] = i
-            return found + (key_at < query_at).astype(jnp.int32)
-
-        found = lax.fori_loop(0, SLOTS, note, jnp.int32(0))
+        found = jnp.int32(0)
+        for i in range(SLOTS):
+            slot_core = core if i < Y_SIZE else 1 - core
+            key_at = place_ref[ctx_of(x, i % Y_SIZE, slot_core)]
+            listed[found] = jnp.int32(i)
+            found = found + (key_at < query_at).astype(jnp.int32)
         top[...] = jnp.full_like(top, MASKED)
         total[...] = jnp.zeros_like(total)
         acc[...] = jnp.zeros_like(acc)
@@ -160,7 +156,7 @@
         keep.wait()
 
 
-def merge_kernel(heads, groups, part_ref, own_ref, mate_ref, weight_ref, out_ref,
+def merge_kernel(heads, groups, part_ref, own_ref, mate_ref, weight_ref, mirror_ref, out_ref,
                  hidden, chip, weight, sems):
     features = HEAD_FEATURES
     width = 2 * features
@@ -168,7 +164,10 @@
     core = lax.rem(me, CORES)
     x = lax.div(me, CORES * Y_SIZE)
     copies = [
-        pltpu.make_async_copy(weight_ref.at[j], weight.at[j], sems.at[j]) for j in range(PEERS)
+        pltpu.make_async_copy(
+            source.at[:, i], weight.at[i * CORES + side], sems.at[2 * i + turn])
+        for i in range(X_SIZE)
+        for turn, (source, side) in enumerate(((weight_ref, core), (mirror_ref, 1 - core)))
     ]
     for copy in copies:
         copy.start()
@@ -243,11 +242,11 @@
     turned = out_weight.T
     sent = pl.pallas_call(
         pack_kernel,
-        out_shape=jax.ShapeDtypeStruct((rows + 2 * turned.shape[0], width), jnp.bfloat16),
-        in_specs=[pl.BlockSpec(memory_space=pltpu.VMEM)] * 3,
+        out_shape=jax.ShapeDtypeStruct((rows, width), jnp.bfloat16),
+        in_specs=[pl.BlockSpec(memory_space=pltpu.VMEM)] * 2,
         out_specs=pl.BlockSpec(memory_space=pltpu.VMEM),
         name="pack",
-    )(keys, values, turned)
+    )(keys, values)
     line = lax.all_gather(sent, "ctx", axis=0, axis_index_groups=Y_GROUPS)
 
     asked = jnp.stack([queries[:, c * width:(c + 1) * width] for c in range(CORES)], 0)
@@ -255,12 +254,17 @@
     asked = lax.all_to_all(asked, "ctx", 0, 0, tiled=True, axis_index_groups=XC_GROUPS)
     asked = hold(asked)
     asked = pltpu.with_memory_space_constraint(asked, pltpu.HBM)
+    column = jnp.concatenate([turned[:, :width], turned[:, width:]], 0)
+    column = jnp.broadcast_to(column[None], (X_SIZE,) + column.shape)
+    column = lax.all_to_all(column, "ctx", 0, 0, tiled=True, axis_index_groups=X_GROUPS)
+    column = hold(column)
     swap = [(i, i ^ 1) for i in range(blocks)]
     other = lax.ppermute(line, "ctx", swap)
     held = pltpu.with_memory_space_constraint(line, pltpu.HBM)
-    spread = line[:, rows:]
-    weights = lax.all_gather(spread, "ctx", axis=0, axis_index_groups=XC_GROUPS)
+    weights = lax.all_gather(column, "ctx", axis=0, axis_index_groups=Y_GROUPS)
     weights = pltpu.with_memory_space_constraint(weights, pltpu.HBM)
+    mirrored = lax.ppermute(weights, "ctx", swap)
+    mirrored = pltpu.with_memory_space_constraint(mirrored, pltpu.HBM)
 
     def attend(own, *lines):
         count = CORES if own else PEERS
@@ -305,17 +309,17 @@
         out_shape=jax.ShapeDtypeStruct((groups, rows, out_columns), jnp.bfloat16),
         in_specs=[
             pl.BlockSpec(memory_space=pltpu.VMEM),
-        ] * 3 + [pl.BlockSpec(memory_space=pltpu.HBM)],
+        ] * 3 + [pl.BlockSpec(memory_space=pltpu.HBM)] * 2,
         out_specs=pl.BlockSpec(memory_space=pltpu.VMEM),
         scratch_shapes=[
             pltpu.VMEM((rows, columns), jnp.bfloat16),
             pltpu.VMEM((CORES, width + STAT_ROWS, rows), jnp.bfloat16),
-            pltpu.VMEM(weights.shape, jnp.bfloat16),
+            pltpu.VMEM((PEERS, Y_SIZE) + weights.shape[-2:], jnp.bfloat16),
             pltpu.SemaphoreType.DMA((PEERS,)),
         ],
         compiler_params=pltpu.CompilerParams(vmem_limit_bytes=32 * 1024 * 1024),
         name="merge_project",
-    )(gathered, near, mate, weights)
+    )(gathered, near, mate, weights, mirrored)
     return lax.psum_scatter(
         terms.reshape(groups * rows, out_columns), "head", scatter_dimension=0, tiled=True
     )

time: 181 us -> 202 us (1.12)
  waiting for transfers between devices: 95.6 us -> 122 us
  blocking collectives: 24.4 us -> 10.9 us
  starting transfers between devices: 7.84 us -> 16.3 us
    all_gather x1, waiting for transfers between devices: 0.01 us -> 37.2 us  [body(): weights = lax.all_gather(column, 'ctx', axis=0, axis_index_groups=Y_GROUPS)]
    all_to_all x1, blocking collectives: 24.4 us -> 10.9 us  [body(): lax.all_to_all(column, 'ctx', 0, 0, tiled=True, axis_index_groups=X_GROUPS)]
    all_gather x1, waiting for transfers between devices: 47.4 us -> 34.6 us  [body(): line = lax.all_gather(sent, 'ctx', axis=0, axis_index_groups=Y_GROUPS)]
    all_to_all x0 -> x1, starting transfers between devices: none -> 4.2 us  [body(): lax.all_to_all(asked, 'ctx', 0, 0, tiled=True, axis_index_groups=XC_GROUPS)]
    all_to_all x1, starting transfers between devices: 3.57 us -> 5.88 us  [body(): lax.all_to_all(parts, 'ctx', 0, 0, tiled=True, axis_index_groups=XC_GROUPS)]
  transfers between devices with their start and end apart: 6 -> 8, of which waited for: 4 -> 5; matrix products, arithmetic and copies ran while one was open for 0% -> 1% of each run, Pallas kernels for 17% -> 14%
where the time goes in v6:
time: 202 us
  waiting for transfers between devices  122 us (60%)
  Pallas kernels  35.4 us (18%)
  starting transfers between devices  16.3 us (8%)
  between operations  13.2 us (7%)
  blocking collectives  10.9 us (5%)
  local copies, waits for them, and re-layouts  3.92 us (2%)
    reduce_scatter x1, waiting for transfers between devices, body(): lax.psum_scatter(terms.reshape(groups * rows, out_columns), 'head', scatt...  44 us
    all_gather x1, waiting for transfers between devices, body(): weights = lax.all_gather(column, 'ctx', axis=0, axis_index_groups=Y_GROUPS)  37.2 us
    all_gather x1, waiting for transfers between devices, body(): line = lax.all_gather(sent, 'ctx', axis=0, axis_index_groups=Y_GROUPS)  34.6 us
    pallas_call x2, Pallas kernels, attend(): pl.pallas_call(functools.partial(attend_kernel, own, rows, heads), out_sh...  28.9 us
    all_to_all x1, blocking collectives, body(): lax.all_to_all(column, 'ctx', 0, 0, tiled=True, axis_index_groups=X_GROUPS)  10.9 us
    all_to_all x1, starting transfers between devices, body(): lax.all_to_all(parts, 'ctx', 0, 0, tiled=True, axis_index_groups=XC_GROUPS)  5.88 us
    all_to_all x1, waiting for transfers between devices, body(): lax.all_to_all(parts, 'ctx', 0, 0, tiled=True, axis_index_groups=XC_GROUPS)  4.96 us
    pallas_call x1, Pallas kernels, body(): pl.pallas_call(functools.partial(merge_kernel, heads, groups), out_shape=...  4.78 us
  transfers between devices with their start and end apart: 8, of which 5 were waited for; matrix products, arithmetic and copies ran while one was open for 1% of the time, Pallas kernels for 14%

profile of v6, /device:TPU:8, one launch (start us, length us, event | category | flops | bytes accessed | tf_op | source)
XLA Modules:
  0.0 201.6 jit_solution(11097445902639010924)
XLA Ops:
  6.5 0.0 copy-start.2
  6.5 0.0 all-gather.5.cloned.1.call-start
  6.5 1.7 pack.1
  8.2 0.0 all-gather.5.cloned.1.call-update
  8.2 0.0 all-gather.7.cloned.1.call-start
  8.3 0.8 fusion
  9.1 10.9 %all_to_all.15.array_ref = bf16[4,128,256]{2,1,0:T(8,128)(2,1)} all-to-all(bf16[4,128,256]{2,1,0:T(8,128)(2,1)S(1)} %broadcast_in_dim.5), channel_id=1, replica_groups={{0,128,256,384},{8,136,264,392},{16,144,272,400},{24,152,280,408},{32,1..., dimensions={0} | all-to-all | bytes 524288 | tf_op jit(solution)/shard_map/all_to_all | solution.py:259
  20.0 0.0 all-gather.7.cloned.1.call-update
  20.0 34.6 %all-gather.5.cloned.1.call-done = bf16[2048,256]{1,0:T(8,128)(2,1)} async-done(((bf16[256,256]{1,0:T(8,128)(2,1)}), bf16[2048,256]{1,0:T(8,128)(2,1)}) %all-gather.5.cloned.1.call-update) | async-done | bytes 1048592 | tf_op jit(solution)/shard_map/all_gather | solution.py:250
  54.6 1.9 collective-permute-start
  56.5 0.0 copy-done.2
  56.6 1.0 broadcast_in_dim.4
  57.6 4.2 %all-to-all-start = ((bf16[8,256,256]{2,1,0:T(8,128)(2,1)}), bf16[8,256,256]{2,1,0:T(8,128)(2,1)S(1)}, u32[]{:S(2)}, u32[]{:S(2)}) async-start(bf16[8,256,256]{2,1,0:T(8,128)(2,1)} %bitcast.2), calls=%async_computation | async-start | bytes 2097152 | tf_op jit(solution)/shard_map/all_to_all | solution.py:254
  61.8 37.2 %all-gather.7.cloned.1.call-done = bf16[32,128,256]{2,1,0:T(8,128)(2,1)} async-done(((bf16[4,128,256]{2,1,0:T(8,128)(2,1)}), bf16[32,128,256]{2,1,0:T(8,128)(2,1)}) %all-gather.7.cloned.1.call-update) | async-done | bytes 2097168 | tf_op jit(solution)/shard_map/all_gather | solution.py:264
  99.1 1.9 collective-permute-start.2
  101.0 0.0 all-to-all-done.array_ref
  101.0 0.0 copy-start.1
  101.0 1.0 copy-done.1
  102.0 0.0 collective-permute-done.refs_1_
  102.0 0.0 copy-start.3
  102.0 1.0 copy-done.3
  103.0 20.7 %shard_map.55 = (bf16[8,272,256]{2,1,0:T(8,128)(2,1)}, bf16[16,256,256]{2,1,0:T(8,128)(2,1)}) custom-call(s32[64]{0:T(128)} %place_ref.3, bf16[8,256,256]{2,1,0:T(8,128)(2,1)} %hold.2.ask_ref, bf16[8,256,256]{2,1,0:T(8,128)(2,1)} %bitcast.13, bf16[8,256,256]{2,1,0:T(8,128)(2,1)} %copy-done.3), custom_call_target="tpu_custom_call" | custom-call | flops 8000000000 | bytes 5000000 | tf_op jit(solution)/shard_map/pallas_call | solution.py:276
  123.7 0.0 copy-start
  123.7 5.9 %all-to-all-start.1 = ((bf16[8,272,256]{2,1,0:T(8,128)(2,1)}), bf16[8,272,256]{2,1,0:T(8,128)(2,1)S(1)}, u32[]{:S(2)}, u32[]{:S(2)}) async-start(bf16[8,272,256]{2,1,0:T(8,128)(2,1)} %get-tuple-element.7), calls=%async_computation.1 | async-start | bytes 2228224 | tf_op jit(solution)/shard_map/all_to_all | solution.py:302
  129.6 0.0 reduce-scatter.2.cloned.1.call-start
  129.7 0.0 copy-done
  129.7 8.2 %shard_map.56.own_ref = bf16[2,272,256]{2,1,0:T(8,128)(2,1)S(1)} custom-call(s32[64]{0:T(128)S(1)} %copy-done, bf16[8,256,256]{2,1,0:T(8,128)(2,1)} %hold.2.ask_ref, bf16[16,256,256]{2,1,0:T(8,128)(2,1)} %get-tuple-element.8.refs_0_), custom_call_target="tpu_custom_call" | custom-call | flops 2000000000 | bytes 5000000 | tf_op jit(solution)/shard_map/pallas_call | solution.py:276
  137.9 2.4 %collective-permute-start.1 = (bf16[1,272,256]{2,1,0:T(8,128)(2,1)S(1)}, bf16[1,272,256]{2,1,0:T(8,128)(2,1)S(1)}, u32[]{:S(2)}, u32[]{:S(2)}) collective-permute-start(bf16[1,272,256]{2,1,0:T(8,128)(2,1)S(1)} %slice.20), channel_id=1, source_target_pairs={{0,8},{8,0},{16,24},{24,16},{32,40},{40,32},{48,56},{56,48},{64,72... | collective-permute-start | bytes 417800 | tf_op jit(solution)/shard_map/ppermute | solution.py:304
  140.3 1.0 collective-permute-done.1.mate_ref
  141.3 5.0 %all-to-all-done.1.part_ref = bf16[8,272,256]{2,1,0:T(8,128)(2,1)S(1)} async-done(((bf16[8,272,256]{2,1,0:T(8,128)(2,1)}), bf16[8,272,256]{2,1,0:T(8,128)(2,1)S(1)}, u32[]{:S(2)}, u32[]{:S(2)}) %all-to-all-start.1) | async-done | bytes 1114144 | tf_op jit(solution)/shard_map/all_to_all | solution.py:302
  146.2 0.0 collective-permute-done.2.mirror_ref
  146.2 4.8 %merge_project.1 = bf16[8,256,512]{2,1,0:T(8,128)(2,1)} custom-call(bf16[8,272,256]{2,1,0:T(8,128)(2,1)S(1)} %all-to-all-done.1.part_ref, bf16[2,272,256]{2,1,0:T(8,128)(2,1)S(1)} %shard_map.56.own_ref, bf16[1,272,256]{2,1,0:T(8,128)(2,1)S(1)} %collective-permute-done.1.mate_ref, bf16[8,4,128,256]{3,2,1,0:T(8,128)(2,1)} %bitcast.10, ...), custom_call_target="tpu_custom_call" | custom-call | tf_op jit(solution)/shard_map/merge_project/pallas_call | solution.py:307
  151.0 0.0 reduce-scatter.2.cloned.1.call-update
  151.1 44.0 %reduce-scatter.2.cloned.1.call-done = bf16[256,512]{1,0:T(8,128)(2,1)} async-done(((bf16[2048,512]{1,0:T(8,128)(2,1)}), bf16[256,512]{1,0:T(8,128)(2,1)}) %reduce-scatter.2.cloned.1.call-update) | async-done | bytes 262160 | tf_op jit(solution)/shard_map/reduce_scatter | solution.py:323
  (7 shorter events, 0.1 us)
Async XLA Ops:
  6.5 50.0 %copy-start.2 = (bf16[256,512]{1,0:T(8,128)(2,1)S(1)}, bf16[256,512]{1,0:T(8,128)(2,1)}, u32[]{:S(2)}) copy-start(bf16[256,512]{1,0:T(8,128)(2,1)} %param.6) | copy-start | bytes 786436
  6.5 48.0 %all-gather.5.cloned.1.call-start = ((), (), s32[]{:S(2)}) async-start(), calls=%async_computation.5 | async-start | bytes 1179648 | tf_op jit(solution)/shard_map/all_gather | solution.py:250
  8.2 90.8 %all-gather.7.cloned.1.call-start = ((), (), s32[]{:S(2)}) async-start(), calls=%async_computation.6 | async-start | bytes 2359296 | tf_op jit(solution)/shard_map/all_gather | solution.py:264
  54.6 47.4 %collective-permute-start = (bf16[8,256,256]{2,1,0:T(8,128)(2,1)}, bf16[8,256,256]{2,1,0:T(8,128)(2,1)S(1)}, u32[]{:S(2)}, u32[]{:S(2)}) collective-permute-start(bf16[8,256,256]{2,1,0:T(8,128)(2,1)} %bitcast.12), channel_id=1, source_target_pairs={{0,8},{8,0},{16,24},{24,16},{32,40},{40,32},{48,56},{56,48},{64,72... | collective-permute-start | bytes 3145736 | tf_op jit(solution)/shard_map/ppermute | solution.py:262
  57.6 43.4 %all-to-all-start = ((bf16[8,256,256]{2,1,0:T(8,128)(2,1)}), bf16[8,256,256]{2,1,0:T(8,128)(2,1)S(1)}, u32[]{:S(2)}, u32[]{:S(2)}) async-start(bf16[8,256,256]{2,1,0:T(8,128)(2,1)} %bitcast.2), calls=%async_computation | async-start | bytes 2097152 | tf_op jit(solution)/shard_map/all_to_all | solution.py:254
  99.1 47.2 %collective-permute-start.2 = (bf16[8,4,128,256]{3,2,1,0:T(8,128)(2,1)}, bf16[8,4,128,256]{3,2,1,0:T(8,128)(2,1)}, u32[]{:S(2)}, u32[]{:S(2)}) collective-permute-start(bf16[8,4,128,256]{3,2,1,0:T(8,128)(2,1)} %bitcast.9), channel_id=1, source_target_pairs={{0,8},{8,0},{16,24},{24,16},{32,40},{40,32},{48,56},{56,48},{64,72... | collective-permute-start | bytes 6291464 | tf_op jit(solution)/shard_map/ppermute | solution.py:266
  101.0 1.0 copy-start.1
  102.0 1.0 copy-start.3
  123.7 5.9 %copy-start = (s32[64]{0:T(128)S(1)}, s32[64]{0:T(128)}, u32[]{:S(2)}) copy-start(s32[64]{0:T(128)} %place_ref.3) | copy-start | bytes 772
  123.7 22.5 %all-to-all-start.1 = ((bf16[8,272,256]{2,1,0:T(8,128)(2,1)}), bf16[8,272,256]{2,1,0:T(8,128)(2,1)S(1)}, u32[]{:S(2)}, u32[]{:S(2)}) async-start(bf16[8,272,256]{2,1,0:T(8,128)(2,1)} %get-tuple-element.7), calls=%async_computation.1 | async-start | bytes 2228224 | tf_op jit(solution)/shard_map/all_to_all | solution.py:302
  129.6 65.4 %reduce-scatter.2.cloned.1.call-start = ((), (), s32[]{:S(2)}) async-start(), calls=%async_computation.4 | async-start | bytes 2359296 | tf_op jit(solution)/shard_map/reduce_scatter | solution.py:323
  137.9 3.3 %collective-permute-start.1 = (bf16[1,272,256]{2,1,0:T(8,128)(2,1)S(1)}, bf16[1,272,256]{2,1,0:T(8,128)(2,1)S(1)}, u32[]{:S(2)}, u32[]{:S(2)}) collective-permute-start(bf16[1,272,256]{2,1,0:T(8,128)(2,1)S(1)} %slice.20), channel_id=1, source_target_pairs={{0,8},{8,0},{16,24},{24,16},{32,40},{40,32},{48,56},{56,48},{64,72... | collective-permute-start | bytes 417800 | tf_op jit(solution)/shard_map/ppermute | solution.py:304
Sparse Core Ops, SparseCore 0:
  9.4 45.1 all-gather.4
  56.7 42.3 all-gather.6
  151.2 43.8 reduce-scatter.1

commit v7 on v6

--- a/solution.py
+++ b/solution.py
@@ -26,13 +26,17 @@
 XC_GROUPS = [[ctx_of(x, y, c) for x in range(X_SIZE) for c in range(CORES)] for y in range(Y_SIZE)]
 
 
-def pack_kernel(key_ref, value_ref, out_ref):
+def pack_kernel(key_ref, value_ref, weight_ref, out_ref):
     rows, features = key_ref.shape
     half = rows // 2
+    count = weight_ref.shape[0]
     width = out_ref.shape[1]
     out_ref[0:half, 0:features] = key_ref[0:half, :]
     out_ref[0:half, features:width] = key_ref[half:rows, :]
     out_ref[half:rows, :] = value_ref[...].astype(jnp.float32).T.astype(jnp.bfloat16)
+    for i in range(2):
+        out_ref[rows + i * count:rows + (i + 1) * count, :] = (
+            weight_ref[:, i * width:(i + 1) * width])
 
 
 def attend_kernel(own, rows, heads, place_ref, ask_ref, *refs):
@@ -50,9 +54,9 @@
         line_ref, other_ref, out_ref, kept_ref, listed, q_ref, kv, top, total, acc, kv_sem = refs
         copies = [
             pltpu.make_async_copy(
-                line_ref, kv.at[pl.ds(0, Y_SIZE)], kv_sem.at[0]),
+                line_ref.at[:, pl.ds(0, rows), :], kv.at[pl.ds(0, Y_SIZE)], kv_sem.at[0]),
             pltpu.make_async_copy(
-                other_ref, kv.at[pl.ds(Y_SIZE, Y_SIZE)], kv_sem.at[1]),
+                other_ref.at[:, pl.ds(0, rows), :], kv.at[pl.ds(Y_SIZE, Y_SIZE)], kv_sem.at[1]),
         ]
     copies.append(pltpu.make_async_copy(ask_ref, q_ref, kv_sem.at[2]))
     for copy in copies:
@@ -156,19 +160,25 @@
         keep.wait()
 
 
-def merge_kernel(heads, groups, part_ref, own_ref, mate_ref, weight_ref, mirror_ref, out_ref,
+def merge_kernel(rows, heads, groups, part_ref, own_ref, mate_ref, line_ref, other_ref,
+                 weight_ref, mirror_ref, out_ref,
                  hidden, chip, weight, sems):
     features = HEAD_FEATURES
     width = 2 * features
     me = lax.axis_index("ctx")
     core = lax.rem(me, CORES)
     x = lax.div(me, CORES * Y_SIZE)
+    count = weight.shape[3]
     copies = [
         pltpu.make_async_copy(
-            source.at[:, i], weight.at[i * CORES + side], sems.at[2 * i + turn])
-        for i in range(X_SIZE)
-        for turn, (source, side) in enumerate(((weight_ref, core), (mirror_ref, 1 - core)))
+            line_ref.at[:, pl.ds(rows, count), :], weight.at[0, core], sems.at[0]),
+        pltpu.make_async_copy(
+            other_ref.at[:, pl.ds(rows, count), :], weight.at[0, 1 - core], sems.at[1]),
     ]
+    for i in range(1, X_SIZE):
+        for turned, (source, side) in enumerate(((weight_ref, core), (mirror_ref, 1 - core))):
+            copies.append(pltpu.make_async_copy(
+                source.at[:, i - 1], weight.at[i, side], sems.at[2 * i + turned]))
     for copy in copies:
         copy.start()
     chip[core] = own_ref[0]
@@ -200,25 +210,23 @@
 
     lines = X_SIZE * Y_SIZE // groups
     parts = Y_SIZE // lines
-    part_rows = weight.shape[2] // 2
-    for g in range(groups):
-        if g % parts == 0:
-            for c in range(CORES):
-                copies[(g // parts) * CORES + c].wait()
-        term = None
-        for side in range(2):
-            start = (g % parts) * lines
-            piece = jnp.concatenate([
-                weight[(g // parts) * CORES + c, start + line,
-                           side * part_rows:(side + 1) * part_rows, :]
-                for line in range(lines) for c in range(CORES)
-            ], 0)
-            product = lax.dot_general(
-                hidden[:, side * width:(side + 1) * width], piece,
-                (((1,), (1,)), ((), ())), preferred_element_type=jnp.float32,
-            )
-            term = product if term is None else term + product
-        out_ref[g] = term.astype(jnp.bfloat16)
+    part_rows = count // 2
+    for i in range(X_SIZE):
+        for copy in copies[2 * i:2 * i + 2]:
+            copy.wait()
+        for p in range(parts):
+            term = None
+            for side in range(2):
+                piece = jnp.concatenate([
+                    weight[i, c, p * lines + line, side * part_rows:(side + 1) * part_rows, :]
+                    for line in range(lines) for c in range(CORES)
+                ], 0)
+                product = lax.dot_general(
+                    hidden[:, side * width:(side + 1) * width], piece,
+                    (((1,), (1,)), ((), ())), preferred_element_type=jnp.float32,
+                )
+                term = product if term is None else term + product
+            out_ref[lax.rem(x + i, X_SIZE) * parts + p] = term.astype(jnp.bfloat16)
 
 
 def hold(array):
@@ -232,6 +240,22 @@
     )(array)
 
 
+def turn_kernel(column_ref, out_ref):
+    x = lax.div(lax.axis_index("ctx"), CORES * Y_SIZE)
+    for i in range(X_SIZE - 1):
+        out_ref[i] = column_ref[lax.rem(x + 1 + i, X_SIZE)]
+
+
+def turn(column):
+    return pl.pallas_call(
+        turn_kernel,
+        out_shape=jax.ShapeDtypeStruct((X_SIZE - 1,) + column.shape[1:], column.dtype),
+        in_specs=[pl.BlockSpec(memory_space=pltpu.VMEM)],
+        out_specs=pl.BlockSpec(memory_space=pltpu.VMEM),
+        name="turn",
+    )(column)
+
+
 def body(placement, queries, keys, values, out_weight):
     rows, columns = queries.shape
     blocks = placement.shape[0]
@@ -242,11 +266,11 @@
     turned = out_weight.T
     sent = pl.pallas_call(
         pack_kernel,
-        out_shape=jax.ShapeDtypeStruct((rows, width), jnp.bfloat16),
-        in_specs=[pl.BlockSpec(memory_space=pltpu.VMEM)] * 2,
+        out_shape=jax.ShapeDtypeStruct((rows + 2 * turned.shape[0], width), jnp.bfloat16),
+        in_specs=[pl.BlockSpec(memory_space=pltpu.VMEM)] * 3,
         out_specs=pl.BlockSpec(memory_space=pltpu.VMEM),
         name="pack",
-    )(keys, values)
+    )(keys, values, turned)
     line = lax.all_gather(sent, "ctx", axis=0, axis_index_groups=Y_GROUPS)
 
     asked = jnp.stack([queries[:, c * width:(c + 1) * width] for c in range(CORES)], 0)
@@ -257,7 +281,7 @@
     column = jnp.concatenate([turned[:, :width], turned[:, width:]], 0)
     column = jnp.broadcast_to(column[None], (X_SIZE,) + column.shape)
     column = lax.all_to_all(column, "ctx", 0, 0, tiled=True, axis_index_groups=X_GROUPS)
-    column = hold(column)
+    column = turn(column)
     swap = [(i, i ^ 1) for i in range(blocks)]
     other = lax.ppermute(line, "ctx", swap)
     held = pltpu.with_memory_space_constraint(line, pltpu.HBM)
@@ -301,25 +325,25 @@
     kept = pltpu.with_memory_space_constraint(kept, pltpu.HBM)
     gathered = lax.all_to_all(parts, "ctx", 0, 0, tiled=True, axis_index_groups=XC_GROUPS)
     near, = attend(True, kept)
-    mate = lax.ppermute(near[1:], "ctx", swap)
+    mate = hold(lax.ppermute(near[1:], "ctx", swap))
 
     out_columns = blocks * turned.shape[0] // groups
     terms = pl.pallas_call(
-        functools.partial(merge_kernel, heads, groups),
+        functools.partial(merge_kernel, rows, heads, groups),
         out_shape=jax.ShapeDtypeStruct((groups, rows, out_columns), jnp.bfloat16),
         in_specs=[
             pl.BlockSpec(memory_space=pltpu.VMEM),
-        ] * 3 + [pl.BlockSpec(memory_space=pltpu.HBM)] * 2,
+        ] * 3 + [pl.BlockSpec(memory_space=pltpu.HBM)] * 4,
         out_specs=pl.BlockSpec(memory_space=pltpu.VMEM),
         scratch_shapes=[
             pltpu.VMEM((rows, columns), jnp.bfloat16),
             pltpu.VMEM((CORES, width + STAT_ROWS, rows), jnp.bfloat16),
-            pltpu.VMEM((PEERS, Y_SIZE) + weights.shape[-2:], jnp.bfloat16),
+            pltpu.VMEM((X_SIZE, CORES, Y_SIZE) + weights.shape[-2:], jnp.bfloat16),
             pltpu.SemaphoreType.DMA((PEERS,)),
         ],
         compiler_params=pltpu.CompilerParams(vmem_limit_bytes=32 * 1024 * 1024),
         name="merge_project",
-    )(gathered, near, mate, weights, mirrored)
+    )(gathered, near, mate, held, other, weights, mirrored)
     return lax.psum_scatter(
         terms.reshape(groups * rows, out_columns), "head", scatter_dimension=0, tiled=True
     )

time: 202 us -> 202 us (level)
  the two profiles are of different devices: /device:TPU:8 before, /device:TPU:2 now
where the time goes in v7:
time: 202 us; the launch traced here: 201 us
  waiting for transfers between devices  106 us (52%)
  Pallas kernels  34.4 us (17%)
  blocking collectives  33.6 us (17%)
  between operations  13.3 us (7%)
  starting transfers between devices  9.87 us (5%)
  local copies, waits for them, and re-layouts  3.67 us (2%)
    reduce_scatter x1, waiting for transfers between devices, body(): lax.psum_scatter(terms.reshape(groups * rows, out_columns), 'head', scatt...  47.8 us
    all_gather x1, waiting for transfers between devices, body(): line = lax.all_gather(sent, 'ctx', axis=0, axis_index_groups=Y_GROUPS)  31.1 us
    pallas_call x2, Pallas kernels, attend(): pl.pallas_call(functools.partial(attend_kernel, own, rows, heads), out_sh...  26.7 us
    all_gather x1, waiting for transfers between devices, body(): weights = lax.all_gather(column, 'ctx', axis=0, axis_index_groups=Y_GROUPS)  21.5 us
    all_to_all x1, blocking collectives, body(): lax.all_to_all(asked, 'ctx', 0, 0, tiled=True, axis_index_groups=XC_GROUPS)  19.4 us
    all_to_all x1, blocking collectives, body(): lax.all_to_all(column, 'ctx', 0, 0, tiled=True, axis_index_groups=X_GROUPS)  14.2 us
    all_to_all x1, waiting for transfers between devices, body(): lax.all_to_all(parts, 'ctx', 0, 0, tiled=True, axis_index_groups=XC_GROUPS)  4.76 us
    pallas_call x1, Pallas kernels, body(): pl.pallas_call(functools.partial(merge_kernel, rows, heads, groups), out_...  4.36 us
  transfers between devices with their start and end apart: 7, of which 5 were waited for; matrix products, arithmetic and copies ran while one was open for 0% of the time, Pallas kernels for 14%

profile of v7, /device:TPU:2, one launch (start us, length us, event | category | flops | bytes accessed | tf_op | source)
XLA Modules:
  0.0 201.1 jit_solution(15205705804059925426)
XLA Ops:
  6.5 0.0 copy-start.5
  6.5 0.0 all-gather.5.cloned.1.call-start
  6.5 1.7 pack.1
  8.3 0.0 all-gather.5.cloned.1.call-update
  8.3 0.0 all-gather.7.cloned.1.call-start
  8.3 0.8 fusion
  9.2 14.2 %all_to_all.15.column_ref = bf16[4,128,256]{2,1,0:T(8,128)(2,1)} all-to-all(bf16[4,128,256]{2,1,0:T(8,128)(2,1)S(1)} %broadcast_in_dim.5), channel_id=1, replica_groups={{0,128,256,384},{8,136,264,392},{16,144,272,400},{24,152,280,408},{32,1..., dimensions={0} | all-to-all | bytes 524288 | tf_op jit(solution)/shard_map/all_to_all | solution.py:283
  23.3 1.6 turn.1
  24.9 0.0 all-gather.7.cloned.1.call-update
  25.0 31.1 %all-gather.5.cloned.1.call-done = bf16[3072,256]{1,0:T(8,128)(2,1)} async-done(((bf16[384,256]{1,0:T(8,128)(2,1)}), bf16[3072,256]{1,0:T(8,128)(2,1)}) %all-gather.5.cloned.1.call-update) | async-done | bytes 1572880 | tf_op jit(solution)/shard_map/all_gather | solution.py:274
  56.1 1.9 collective-permute-start
  58.0 0.0 copy-done.5
  58.1 0.1 broadcast_in_dim.4
  58.1 19.4 %all_to_all.16.array_ref = bf16[8,256,256]{2,1,0:T(8,128)(2,1)} all-to-all(bf16[8,256,256]{2,1,0:T(8,128)(2,1)S(1)} %bitcast.9), channel_id=1, replica_groups={{0,8,128,136,256,264,384,392},{16,24,144,152,272,280,400,408},{32,40,16..., dimensions={0} | all-to-all | bytes 2097152 | tf_op jit(solution)/shard_map/all_to_all | solution.py:278
  77.6 21.5 %all-gather.7.cloned.1.call-done = bf16[24,128,256]{2,1,0:T(8,128)(2,1)} async-done(((bf16[3,128,256]{2,1,0:T(8,128)(2,1)}), bf16[24,128,256]{2,1,0:T(8,128)(2,1)}) %all-gather.7.cloned.1.call-update) | async-done | bytes 1572880 | tf_op jit(solution)/shard_map/all_gather | solution.py:288
  99.1 1.9 collective-permute-start.2
  101.0 0.0 collective-permute-done.refs_1_.other_ref
  101.0 0.0 copy-start
  101.0 1.2 copy-done
  102.2 20.5 %shard_map.55 = (bf16[8,272,256]{2,1,0:T(8,128)(2,1)}, bf16[16,256,256]{2,1,0:T(8,128)(2,1)}) custom-call(s32[64]{0:T(128)} %place_ref.3, bf16[8,256,256]{2,1,0:T(8,128)(2,1)} %hold.2.ask_ref, bf16[8,384,256]{2,1,0:T(8,128)(2,1)} %bitcast.11, bf16[8,384,256]{2,1,0:T(8,128)(2,1)} %copy-done), custom_call_target="tpu_custom_call" | custom-call | flops 8000000000 | bytes 5000000 | tf_op jit(solution)/shard_map/pallas_call | solution.py:300
  122.8 0.0 copy-start.4
  122.8 3.5 %all-to-all-start.1 = ((bf16[8,272,256]{2,1,0:T(8,128)(2,1)}), bf16[8,272,256]{2,1,0:T(8,128)(2,1)S(1)}, u32[]{:S(2)}, u32[]{:S(2)}) async-start(bf16[8,272,256]{2,1,0:T(8,128)(2,1)} %get-tuple-element.7), calls=%async_computation.1 | async-start | bytes 2228224 | tf_op jit(solution)/shard_map/all_to_all | solution.py:326
  126.3 0.0 reduce-scatter.2.cloned.1.call-start
  126.3 0.0 copy-done.4
  126.4 0.0 copy-start.1
  126.4 6.1 %shard_map.56.own_ref = bf16[2,272,256]{2,1,0:T(8,128)(2,1)S(1)} custom-call(s32[64]{0:T(128)S(1)} %copy-done.4, bf16[8,256,256]{2,1,0:T(8,128)(2,1)} %hold.2.ask_ref, bf16[16,256,256]{2,1,0:T(8,128)(2,1)} %get-tuple-element.8.refs_0_), custom_call_target="tpu_custom_call" | custom-call | flops 2000000000 | bytes 5000000 | tf_op jit(solution)/shard_map/pallas_call | solution.py:300
  132.5 2.4 %collective-permute-start.1 = (bf16[1,272,256]{2,1,0:T(8,128)(2,1)S(1)}, bf16[1,272,256]{2,1,0:T(8,128)(2,1)S(1)}, u32[]{:S(2)}, u32[]{:S(2)}) collective-permute-start(bf16[1,272,256]{2,1,0:T(8,128)(2,1)S(1)} %slice.20), channel_id=1, source_target_pairs={{0,8},{8,0},{16,24},{24,16},{32,40},{40,32},{48,56},{56,48},{64,72... | collective-permute-start | bytes 417800 | tf_op jit(solution)/shard_map/ppermute | solution.py:328
  135.0 1.0 collective-permute-done.1.array_ref
  136.0 0.0 copy-start.2
  136.0 0.7 copy-done.2
  136.6 0.0 collective-permute-done.2.mirror_ref
  136.6 4.8 %all-to-all-done.1.part_ref = bf16[8,272,256]{2,1,0:T(8,128)(2,1)S(1)} async-done(((bf16[8,272,256]{2,1,0:T(8,128)(2,1)}), bf16[8,272,256]{2,1,0:T(8,128)(2,1)S(1)}, u32[]{:S(2)}, u32[]{:S(2)}) %all-to-all-start.1) | async-done | bytes 1114144 | tf_op jit(solution)/shard_map/all_to_all | solution.py:326
  141.4 0.0 copy-done.1
  141.4 0.0 copy-start.3
  141.4 0.9 copy-done.3
  142.3 4.4 %merge_project.1 = bf16[8,256,512]{2,1,0:T(8,128)(2,1)} custom-call(bf16[8,272,256]{2,1,0:T(8,128)(2,1)S(1)} %all-to-all-done.1.part_ref, bf16[2,272,256]{2,1,0:T(8,128)(2,1)S(1)} %shard_map.56.own_ref, bf16[1,272,256]{2,1,0:T(8,128)(2,1)S(1)} %copy-done.3, bf16[8,384,256]{2,1,0:T(8,128)(2,1)} %bitcast.12, bf16[8,384,256]{2,1,0:T(8,128)(2,1)S(1)} %copy-done.1, ...), custom_call_target="tpu_custom_call" | custom-call | tf_op jit(solution)/shard_map/merge_project/pallas_call | solution.py:331
  146.7 0.0 reduce-scatter.2.cloned.1.call-update
  146.7 47.8 %reduce-scatter.2.cloned.1.call-done = bf16[256,512]{1,0:T(8,128)(2,1)} async-done(((bf16[2048,512]{1,0:T(8,128)(2,1)}), bf16[256,512]{1,0:T(8,128)(2,1)}) %reduce-scatter.2.cloned.1.call-update) | async-done | bytes 262160 | tf_op jit(solution)/shard_map/reduce_scatter | solution.py:347
  (7 shorter events, 0.1 us)
Async XLA Ops:
  6.5 51.5 %copy-start.5 = (bf16[256,512]{1,0:T(8,128)(2,1)S(1)}, bf16[256,512]{1,0:T(8,128)(2,1)}, u32[]{:S(2)}) copy-start(bf16[256,512]{1,0:T(8,128)(2,1)} %param.6) | copy-start | bytes 786436
  6.5 49.5 %all-gather.5.cloned.1.call-start = ((), (), s32[]{:S(2)}) async-start(), calls=%async_computation.5 | async-start | bytes 1769472 | tf_op jit(solution)/shard_map/all_gather | solution.py:274
  8.3 90.8 %all-gather.7.cloned.1.call-start = ((), (), s32[]{:S(2)}) async-start(), calls=%async_computation.6 | async-start | bytes 1769472 | tf_op jit(solution)/shard_map/all_gather | solution.py:288
  56.1 44.9 %collective-permute-start = (bf16[8,384,256]{2,1,0:T(8,128)(2,1)}, bf16[8,384,256]{2,1,0:T(8,128)(2,1)S(1)}, u32[]{:S(2)}, u32[]{:S(2)}) collective-permute-start(bf16[8,384,256]{2,1,0:T(8,128)(2,1)} %bitcast.10), channel_id=1, source_target_pairs={{0,8},{8,0},{16,24},{24,16},{32,40},{40,32},{48,56},{56,48},{64,72... | collective-permute-start | bytes 4718600 | tf_op jit(solution)/shard_map/ppermute | solution.py:286
  99.1 37.5 %collective-permute-start.2 = (bf16[8,3,128,256]{3,2,1,0:T(8,128)(2,1)}, bf16[8,3,128,256]{3,2,1,0:T(8,128)(2,1)}, u32[]{:S(2)}, u32[]{:S(2)}) collective-permute-start(bf16[8,3,128,256]{3,2,1,0:T(8,128)(2,1)} %bitcast.13), channel_id=1, source_target_pairs={{0,8},{8,0},{16,24},{24,16},{32,40},{40,32},{48,56},{56,48},{64,72... | collective-permute-start | bytes 4718600 | tf_op jit(solution)/shard_map/ppermute | solution.py:290
  101.0 1.2 copy-start
  122.8 3.6 %copy-start.4 = (s32[64]{0:T(128)S(1)}, s32[64]{0:T(128)}, u32[]{:S(2)}) copy-start(s32[64]{0:T(128)} %place_ref.3) | copy-start | bytes 772
  122.8 18.6 %all-to-all-start.1 = ((bf16[8,272,256]{2,1,0:T(8,128)(2,1)}), bf16[8,272,256]{2,1,0:T(8,128)(2,1)S(1)}, u32[]{:S(2)}, u32[]{:S(2)}) async-start(bf16[8,272,256]{2,1,0:T(8,128)(2,1)} %get-tuple-element.7), calls=%async_computation.1 | async-start | bytes 2228224 | tf_op jit(solution)/shard_map/all_to_all | solution.py:326
  126.3 68.2 %reduce-scatter.2.cloned.1.call-start = ((), (), s32[]{:S(2)}) async-start(), calls=%async_computation.4 | async-start | bytes 2359296 | tf_op jit(solution)/shard_map/reduce_scatter | solution.py:347
  126.4 15.0 %copy-start.1 = (bf16[8,384,256]{2,1,0:T(8,128)(2,1)S(1)}, bf16[8,384,256]{2,1,0:T(8,128)(2,1)}, u32[]{:S(2)}) copy-start(bf16[8,384,256]{2,1,0:T(8,128)(2,1)} %copy-done) | copy-start | bytes 4718596
  132.5 3.4 %collective-permute-start.1 = (bf16[1,272,256]{2,1,0:T(8,128)(2,1)S(1)}, bf16[1,272,256]{2,1,0:T(8,128)(2,1)S(1)}, u32[]{:S(2)}, u32[]{:S(2)}) collective-permute-start(bf16[1,272,256]{2,1,0:T(8,128)(2,1)S(1)} %slice.20), channel_id=1, source_target_pairs={{0,8},{8,0},{16,24},{24,16},{32,40},{40,32},{48,56},{56,48},{64,72... | collective-permute-start | bytes 417800 | tf_op jit(solution)/shard_map/ppermute | solution.py:328
  136.0 0.7 copy-start.2
  141.4 0.9 copy-start.3
Sparse Core Ops, SparseCore 0:
  9.4 46.6 all-gather.4
  58.2 40.8 all-gather.6
  146.8 47.6 reduce-scatter.1

commit v8 on v7

--- a/solution.py
+++ b/solution.py
@@ -162,7 +162,7 @@
 
 def merge_kernel(rows, heads, groups, part_ref, own_ref, mate_ref, line_ref, other_ref,
                  weight_ref, mirror_ref, out_ref,
-                 hidden, chip, weight, sems):
+                 hidden, chip, weight, sems, near_sems):
     features = HEAD_FEATURES
     width = 2 * features
     me = lax.axis_index("ctx")
@@ -179,10 +179,16 @@
         for turned, (source, side) in enumerate(((weight_ref, core), (mirror_ref, 1 - core))):
             copies.append(pltpu.make_async_copy(
                 source.at[:, i - 1], weight.at[i, side], sems.at[2 * i + turned]))
+    near_copies = [
+        pltpu.make_async_copy(own_ref.at[0], chip.at[core], near_sems.at[0]),
+        pltpu.make_async_copy(mate_ref.at[0], chip.at[1 - core], near_sems.at[1]),
+    ]
+    for copy in near_copies:
+        copy.start()
     for copy in copies:
         copy.start()
-    chip[core] = own_ref[0]
-    chip[1 - core] = mate_ref[0]
+    for copy in near_copies:
+        copy.wait()
 
     for c in range(CORES):
         sources = [chip.at[c]] + [
@@ -326,6 +332,7 @@
     gathered = lax.all_to_all(parts, "ctx", 0, 0, tiled=True, axis_index_groups=XC_GROUPS)
     near, = attend(True, kept)
     mate = hold(lax.ppermute(near[1:], "ctx", swap))
+    mate = pltpu.with_memory_space_constraint(mate, pltpu.HBM)
 
     out_columns = blocks * turned.shape[0] // groups
     terms = pl.pallas_call(
@@ -333,13 +340,14 @@
         out_shape=jax.ShapeDtypeStruct((groups, rows, out_columns), jnp.bfloat16),
         in_specs=[
             pl.BlockSpec(memory_space=pltpu.VMEM),
-        ] * 3 + [pl.BlockSpec(memory_space=pltpu.HBM)] * 4,
+        ] + [pl.BlockSpec(memory_space=pl.ANY)] * 2 + [pl.BlockSpec(memory_space=pltpu.HBM)] * 4,
         out_specs=pl.BlockSpec(memory_space=pltpu.VMEM),
         scratch_shapes=[
             pltpu.VMEM((rows, columns), jnp.bfloat16),
             pltpu.VMEM((CORES, width + STAT_ROWS, rows), jnp.bfloat16),
             pltpu.VMEM((X_SIZE, CORES, Y_SIZE) + weights.shape[-2:], jnp.bfloat16),
             pltpu.SemaphoreType.DMA((PEERS,)),
+            pltpu.SemaphoreType.DMA((2,)),
         ],
         compiler_params=pltpu.CompilerParams(vmem_limit_bytes=32 * 1024 * 1024),
         name="merge_project",

time: 202 us -> 201 us (level)
  the two profiles are of different devices: /device:TPU:2 before, /device:TPU:10 now
where the time goes in v8:
time: 201 us; the launch traced here: 200 us
  waiting for transfers between devices  105 us (52%)
  Pallas kernels  39 us (19%)
  blocking collectives  29.4 us (15%)
  between operations  13.2 us (7%)
  starting transfers between devices  10.5 us (5%)
  local copies, waits for them, and re-layouts  2.77 us (1%)
    reduce_scatter x1, waiting for transfers between devices, body(): lax.psum_scatter(terms.reshape(groups * rows, out_columns), 'head', scatt...  45 us
    all_gather x1, waiting for transfers between devices, body(): line = lax.all_gather(sent, 'ctx', axis=0, axis_index_groups=Y_GROUPS)  34.9 us
    pallas_call x2, Pallas kernels, attend(): pl.pallas_call(functools.partial(attend_kernel, own, rows, heads), out_sh...  31 us
    all_gather x1, waiting for transfers between devices, body(): weights = lax.all_gather(column, 'ctx', axis=0, axis_index_groups=Y_GROUPS)  21.5 us
    all_to_all x1, blocking collectives, body(): lax.all_to_all(asked, 'ctx', 0, 0, tiled=True, axis_index_groups=XC_GROUPS)  19.4 us
    all_to_all x1, blocking collectives, body(): lax.all_to_all(column, 'ctx', 0, 0, tiled=True, axis_index_groups=X_GROUPS)  9.95 us
    pallas_call x1, Pallas kernels, body(): pl.pallas_call(functools.partial(merge_kernel, rows, heads, groups), out_...  4.71 us
    all_to_all x1, starting transfers between devices, body(): lax.all_to_all(parts, 'ctx', 0, 0, tiled=True, axis_index_groups=XC_GROUPS)  4.64 us
  transfers between devices with their start and end apart: 7, of which 5 were waited for; matrix products, arithmetic and copies ran while one was open for 0% of the time, Pallas kernels for 16%

profile of v8, /device:TPU:10, one launch (start us, length us, event | category | flops | bytes accessed | tf_op | source)
XLA Modules:
  0.0 200.4 jit_solution(11046430428187003994)
XLA Ops:
  6.5 0.0 copy-start.4
  6.5 0.0 all-gather.5.cloned.1.call-start
  6.5 1.7 pack.1
  8.3 0.0 all-gather.5.cloned.1.call-update
  8.3 0.0 all-gather.7.cloned.1.call-start
  8.3 0.8 fusion
  9.2 10.0 %all_to_all.15.column_ref = bf16[4,128,256]{2,1,0:T(8,128)(2,1)} all-to-all(bf16[4,128,256]{2,1,0:T(8,128)(2,1)S(1)} %broadcast_in_dim.5), channel_id=1, replica_groups={{0,128,256,384},{8,136,264,392},{16,144,272,400},{24,152,280,408},{32,1..., dimensions={0} | all-to-all | bytes 524288 | tf_op jit(solution)/shard_map/all_to_all | solution.py:289
  19.1 1.6 turn.1
  20.7 0.0 all-gather.7.cloned.1.call-update
  20.8 34.9 %all-gather.5.cloned.1.call-done = bf16[3072,256]{1,0:T(8,128)(2,1)} async-done(((bf16[384,256]{1,0:T(8,128)(2,1)}), bf16[3072,256]{1,0:T(8,128)(2,1)}) %all-gather.5.cloned.1.call-update) | async-done | bytes 1572880 | tf_op jit(solution)/shard_map/all_gather | solution.py:280
  55.7 1.9 collective-permute-start
  57.6 0.0 copy-done.4
  57.7 0.1 broadcast_in_dim.4
  57.8 19.4 %all_to_all.16.array_ref = bf16[8,256,256]{2,1,0:T(8,128)(2,1)} all-to-all(bf16[8,256,256]{2,1,0:T(8,128)(2,1)S(1)} %bitcast.9), channel_id=1, replica_groups={{0,8,128,136,256,264,384,392},{16,24,144,152,272,280,400,408},{32,40,16..., dimensions={0} | all-to-all | bytes 2097152 | tf_op jit(solution)/shard_map/all_to_all | solution.py:284
  77.2 21.5 %all-gather.7.cloned.1.call-done = bf16[24,128,256]{2,1,0:T(8,128)(2,1)} async-done(((bf16[3,128,256]{2,1,0:T(8,128)(2,1)}), bf16[24,128,256]{2,1,0:T(8,128)(2,1)}) %all-gather.7.cloned.1.call-update) | async-done | bytes 1572880 | tf_op jit(solution)/shard_map/all_gather | solution.py:294
  98.7 1.9 collective-permute-start.2
  100.6 0.0 collective-permute-done.refs_1_.other_ref
  100.6 0.0 copy-start
  100.6 1.2 copy-done
  101.8 22.5 %shard_map.55 = (bf16[8,272,256]{2,1,0:T(8,128)(2,1)}, bf16[16,256,256]{2,1,0:T(8,128)(2,1)}) custom-call(s32[64]{0:T(128)} %place_ref.3, bf16[8,256,256]{2,1,0:T(8,128)(2,1)} %hold.2.ask_ref, bf16[8,384,256]{2,1,0:T(8,128)(2,1)} %bitcast.11, bf16[8,384,256]{2,1,0:T(8,128)(2,1)} %copy-done), custom_call_target="tpu_custom_call" | custom-call | flops 8000000000 | bytes 5000000 | tf_op jit(solution)/shard_map/pallas_call | solution.py:306
  124.4 0.0 copy-start.2
  124.4 4.6 %all-to-all-start.1 = ((bf16[8,272,256]{2,1,0:T(8,128)(2,1)}), bf16[8,272,256]{2,1,0:T(8,128)(2,1)S(1)}, u32[]{:S(2)}, u32[]{:S(2)}) async-start(bf16[8,272,256]{2,1,0:T(8,128)(2,1)} %get-tuple-element.7), calls=%async_computation.1 | async-start | bytes 2228224 | tf_op jit(solution)/shard_map/all_to_all | solution.py:332
  129.0 0.0 reduce-scatter.2.cloned.1.call-start
  129.0 0.0 copy-done.2
  129.0 0.0 copy-start.1
  129.0 8.4 %shard_map.56.own_ref = bf16[2,272,256]{2,1,0:T(8,128)(2,1)S(1)} custom-call(s32[64]{0:T(128)S(1)} %copy-done.2, bf16[8,256,256]{2,1,0:T(8,128)(2,1)} %hold.2.ask_ref, bf16[16,256,256]{2,1,0:T(8,128)(2,1)} %get-tuple-element.8.refs_0_), custom_call_target="tpu_custom_call" | custom-call | flops 2000000000 | bytes 5000000 | tf_op jit(solution)/shard_map/pallas_call | solution.py:306
  137.5 2.0 collective-permute-start.1
  139.5 1.2 collective-permute-done.1.array_ref
  140.8 0.0 copy-start.3
  140.8 0.7 copy-done.3
  141.4 0.0 collective-permute-done.2.mirror_ref
  141.4 2.8 %all-to-all-done.1.part_ref = bf16[8,272,256]{2,1,0:T(8,128)(2,1)S(1)} async-done(((bf16[8,272,256]{2,1,0:T(8,128)(2,1)}), bf16[8,272,256]{2,1,0:T(8,128)(2,1)S(1)}, u32[]{:S(2)}, u32[]{:S(2)}) %all-to-all-start.1) | async-done | bytes 1114144 | tf_op jit(solution)/shard_map/all_to_all | solution.py:332
  144.2 0.0 copy-done.1
  144.2 4.7 %merge_project.1 = bf16[8,256,512]{2,1,0:T(8,128)(2,1)} custom-call(bf16[8,272,256]{2,1,0:T(8,128)(2,1)S(1)} %all-to-all-done.1.part_ref, bf16[2,272,256]{2,1,0:T(8,128)(2,1)S(1)} %shard_map.56.own_ref, bf16[1,272,256]{2,1,0:T(8,128)(2,1)} %hold.3.mate_ref, bf16[8,384,256]{2,1,0:T(8,128)(2,1)} %bitcast.12, bf16[8,384,256]{2,1,0:T(8,128)(2,1)S(1)} %copy-done.1, ...), custom_call_target="tpu_custom_call" | custom-call | tf_op jit(solution)/shard_map/merge_project/pallas_call | solution.py:338
  148.9 0.0 reduce-scatter.2.cloned.1.call-update
  148.9 45.0 %reduce-scatter.2.cloned.1.call-done = bf16[256,512]{1,0:T(8,128)(2,1)} async-done(((bf16[2048,512]{1,0:T(8,128)(2,1)}), bf16[256,512]{1,0:T(8,128)(2,1)}) %reduce-scatter.2.cloned.1.call-update) | async-done | bytes 262160 | tf_op jit(solution)/shard_map/reduce_scatter | solution.py:355
  (7 shorter events, 0.1 us)
Async XLA Ops:
  6.5 51.1 %copy-start.4 = (bf16[256,512]{1,0:T(8,128)(2,1)S(1)}, bf16[256,512]{1,0:T(8,128)(2,1)}, u32[]{:S(2)}) copy-start(bf16[256,512]{1,0:T(8,128)(2,1)} %param.6) | copy-start | bytes 786436
  6.5 49.2 %all-gather.5.cloned.1.call-start = ((), (), s32[]{:S(2)}) async-start(), calls=%async_computation.5 | async-start | bytes 1769472 | tf_op jit(solution)/shard_map/all_gather | solution.py:280
  8.3 90.4 %all-gather.7.cloned.1.call-start = ((), (), s32[]{:S(2)}) async-start(), calls=%async_computation.6 | async-start | bytes 1769472 | tf_op jit(solution)/shard_map/all_gather | solution.py:294
  55.7 44.9 %collective-permute-start = (bf16[8,384,256]{2,1,0:T(8,128)(2,1)}, bf16[8,384,256]{2,1,0:T(8,128)(2,1)S(1)}, u32[]{:S(2)}, u32[]{:S(2)}) collective-permute-start(bf16[8,384,256]{2,1,0:T(8,128)(2,1)} %bitcast.10), channel_id=1, source_target_pairs={{0,8},{8,0},{16,24},{24,16},{32,40},{40,32},{48,56},{56,48},{64,72... | collective-permute-start | bytes 4718600 | tf_op jit(solution)/shard_map/ppermute | solution.py:292
  98.7 42.7 %collective-permute-start.2 = (bf16[8,3,128,256]{3,2,1,0:T(8,128)(2,1)}, bf16[8,3,128,256]{3,2,1,0:T(8,128)(2,1)}, u32[]{:S(2)}, u32[]{:S(2)}) collective-permute-start(bf16[8,3,128,256]{3,2,1,0:T(8,128)(2,1)} %bitcast.13), channel_id=1, source_target_pairs={{0,8},{8,0},{16,24},{24,16},{32,40},{40,32},{48,56},{56,48},{64,72... | collective-permute-start | bytes 4718600 | tf_op jit(solution)/shard_map/ppermute | solution.py:296
  100.6 1.2 copy-start
  124.4 4.7 %copy-start.2 = (s32[64]{0:T(128)S(1)}, s32[64]{0:T(128)}, u32[]{:S(2)}) copy-start(s32[64]{0:T(128)} %place_ref.3) | copy-start | bytes 772
  124.4 19.8 %all-to-all-start.1 = ((bf16[8,272,256]{2,1,0:T(8,128)(2,1)}), bf16[8,272,256]{2,1,0:T(8,128)(2,1)S(1)}, u32[]{:S(2)}, u32[]{:S(2)}) async-start(bf16[8,272,256]{2,1,0:T(8,128)(2,1)} %get-tuple-element.7), calls=%async_computation.1 | async-start | bytes 2228224 | tf_op jit(solution)/shard_map/all_to_all | solution.py:332
  129.0 64.9 %reduce-scatter.2.cloned.1.call-start = ((), (), s32[]{:S(2)}) async-start(), calls=%async_computation.4 | async-start | bytes 2359296 | tf_op jit(solution)/shard_map/reduce_scatter | solution.py:355
  129.0 15.2 %copy-start.1 = (bf16[8,384,256]{2,1,0:T(8,128)(2,1)S(1)}, bf16[8,384,256]{2,1,0:T(8,128)(2,1)}, u32[]{:S(2)}) copy-start(bf16[8,384,256]{2,1,0:T(8,128)(2,1)} %copy-done) | copy-start | bytes 4718596
  137.5 3.3 %collective-permute-start.1 = (bf16[1,272,256]{2,1,0:T(8,128)(2,1)S(1)}, bf16[1,272,256]{2,1,0:T(8,128)(2,1)S(1)}, u32[]{:S(2)}, u32[]{:S(2)}) collective-permute-start(bf16[1,272,256]{2,1,0:T(8,128)(2,1)S(1)} %slice.20), channel_id=1, source_target_pairs={{0,8},{8,0},{16,24},{24,16},{32,40},{40,32},{48,56},{56,48},{64,72... | collective-permute-start | bytes 417800 | tf_op jit(solution)/shard_map/ppermute | solution.py:334
  140.8 0.7 copy-start.3
Sparse Core Ops, SparseCore 0:
  9.4 46.2 all-gather.4
  57.8 40.8 all-gather.6
  149.1 44.8 reduce-scatter.1
